TPU v7x, 32 devices: a whole 2x2x4 slice. The times are simulated.
32 devices in a mesh: tower: 2 (over x), dp: 4 (over y, core), mp: 4 (over z).
Axes of the slice: x: 2, y: 2, z: 4, core: 2. Of those that a mesh axis runs over, the one named last changes fastest.
Arguments:
- tower_in: bfloat16 [2, 4608, 768], P('tower', ('dp', 'mp')), may hold values from -6 to 6
- out_cot: bfloat16 [2, 4608, 768], P('tower', ('dp', 'mp')), may hold values from -6 to 6
- segment_ids: int32 [72, 64], P('dp'), may hold values from 0 to 3, never falling along the last dimension, each value on 1 to 32 neighbouring positions
- row_image: int32 [72], P('dp'), may hold values from 0 to 1
- attn_qkv: bfloat16 [2, 3, 768, 768], P('tower', None, None, 'mp'), may hold values from -0.21875 to 0.21875
- attn_out: bfloat16 [2, 768, 768], P('tower', 'mp'), may hold values from -0.625 to 0.625
- mlp_in: bfloat16 [2, 768, 3072], P('tower', None, 'mp'), may hold values from -0.21875 to 0.21875
- mlp_out: bfloat16 [2, 3072, 768], P('tower', 'mp'), may hold values from -0.109375 to 0.109375
- cross_proj: bfloat16 [2, 2, 768, 768], P('tower', None, None, 'mp'), may hold values from -0.3125 to 0.3125
- qv_bias: float32 [2, 2, 768], P('tower'), may hold values from -3 to 3
- out_bias: float32 [2, 768], P('tower'), may hold values from -1.75 to 1.75
- mlp_bias_in: float32 [2, 3072], P('tower'), may hold values from -3 to 3
- mlp_bias_out: float32 [2, 768], P('tower'), may hold values from -1.75 to 1.75
- norm_gain: float32 [2, 3, 768], P('tower'), may hold values from 0.25 to 1.75
- norm_bias: float32 [2, 3, 768], P('tower'), may hold values from -1.75 to 1.75
Outputs:
- tower_out: bfloat16 [2, 4608, 768], P('tower', ('dp', 'mp'))
- tower_in_grad: bfloat16 [2, 4608, 768], P('tower', ('dp', 'mp'))
- qkv_grad: float32 [2, 3, 768, 768], P('tower', None, 'dp', 'mp')
- attn_out_grad: float32 [2, 768, 768], P('tower', 'mp', 'dp')
- mlp_in_grad: float32 [2, 768, 3072], P('tower', 'dp', 'mp')
- mlp_out_grad: float32 [2, 3072, 768], P('tower', 'mp', 'dp')
- cross_grad: float32 [2, 2, 768, 768], P('tower', None, 'dp', 'mp')
- qv_bias_grad: float32 [2, 2, 768], P('tower')
- out_bias_grad: float32 [2, 768], P('tower')
- mlp_bias_in_grad: float32 [2, 3072], P('tower')
- mlp_bias_out_grad: float32 [2, 768], P('tower')
- norm_gain_grad: float32 [2, 3, 768], P('tower')
- norm_bias_grad: float32 [2, 3, 768], P('tower')
Inputs may be any that keep to these rules, and one draw needn't show every extreme that they name: `segment_ids`: within a caption row of 64 tokens the numbers never fall. Row r and image i belong to one group where r // 18 == i // 2; row_image counts images within the group.
All inputs are finite; a program needn't handle non-finite values.
Results may differ from a plain program's by a relative error of at most 0.03.
Values may be sent and summed in bfloat16 or wider, within the bound.
A program may use at most 192 MiB of HBM per device.

v0:
```python
import functools
from typing import Any, NamedTuple

import jax
import jax.numpy as jnp
from jax import lax
from jax.experimental import pallas as pl
from jax.experimental.pallas import tpu as pltpu
from jax.sharding import PartitionSpec as P

TOWER = "tower"
DP = "dp"
MP = "mp"
HDIM = 64
PATCH = 576
LTXT = 64
EPS = 1e-06
NEG = -1e30
LANES = 128
MESH = pl.DeviceIdType.MESH
F32 = jnp.float32
BF16 = jnp.bfloat16
VMEM_LIMIT = 60 * 1024 * 1024
TAIL_LIMIT = 67043328


def norm_parts(values):
    center = values - jnp.mean(values, axis=-1, keepdims=True)
    spread = jnp.mean(center * center, axis=-1, keepdims=True)
    scale = lax.rsqrt(spread + EPS)
    return (center * scale, scale)


def norm_rows(values, gain_vec, shift_vec):
    unit, _ = norm_parts(values)
    return unit * gain_vec + shift_vec


def norm_back(values, gain_vec, grad_normed):
    unit, scale = norm_parts(values)
    inner = grad_normed * gain_vec
    mean_one = jnp.mean(inner, axis=-1, keepdims=True)
    mean_two = jnp.mean(inner * unit, axis=-1, keepdims=True)
    back = (inner - mean_one - unit * mean_two) * scale
    return (back, jnp.sum(grad_normed * unit, axis=0), jnp.sum(grad_normed, axis=0))


def gelu_tanh(values):
    return jax.nn.gelu(values, approximate=True)


def dot_rows(left, right):
    return lax.dot_general(left, right, (((1,), (1,)), ((), ())), preferred_element_type=F32)


def dot_first(left, right):
    return lax.dot_general(left, right, (((0,), (0,)), ((), ())), preferred_element_type=F32)


def dot_plain(left, right):
    return lax.dot_general(left, right, (((1,), (0,)), ((), ())), preferred_element_type=F32)


def spots():
    tower = lax.axis_index(TOWER)
    dp = lax.axis_index(DP)
    z = lax.axis_index(MP)
    core = lax.rem(dp, 2)
    line = dp // 2
    return tower, dp, z, core, line, dp + 2 - 4 * line, dp + 1 - 2 * core


def greet(target):
    pl.semaphore_signal(pltpu.get_barrier_semaphore(), inc=1, device_id=target, device_id_type=MESH)


def weight_steps(pieces, srcs, outs, stages, sems):
    send_sem, recv_sem, local_sem, twin_send, twin_recv = sems
    tower, dp, z, core, line, other, partner = spots()
    place = z + core * (3 - 2 * z)
    ahead = z + 1 - 2 * core
    behind = z - 1 + 2 * core
    slot_of = (core, 1 - core)
    holder = place <= 1
    far_src = [k for k, p in enumerate(pieces) if p[7]]

    def spot(piece, slot, half):
        which, first, _, count, start, size, _, _ = piece
        part = size // 2
        return outs[which].at[pl.ds(first, count), slot, pl.ds(start + half * part, part), :]

    def own(piece):
        which, _, first, count, start, size, _, far = piece
        part = size // 2
        if far:
            return spot(piece, lax.rem(z, 2), line)
        return srcs[which].at[pl.ds(first, count), pl.ds(start + line * part, part), :]

    def move(k, source, slot, half, kind, arrive, target):
        return pltpu.make_async_remote_copy(
            src_ref=source,
            dst_ref=spot(pieces[k], slot, half),
            send_sem=send_sem.at[k, kind],
            recv_sem=recv_sem.at[k, arrive],
            device_id=target,
            device_id_type=MESH,
        )

    def twin_copy():
        which = pieces[far_src[0]][0]
        return pltpu.make_async_remote_copy(
            src_ref=srcs[which],
            dst_ref=outs[which].at[pl.ds(0, srcs[which].shape[0]), lax.rem(z, 2)],
            send_sem=twin_send,
            recv_sem=twin_recv,
            device_id={TOWER: 1 - tower},
            device_id_type=MESH,
        )

    def local_in(i):
        return pltpu.make_async_copy(srcs[i], stages[i], local_sem.at[i, 0])

    def local_out(i):
        first = outs[i].shape[0] - srcs[i].shape[0]
        return pltpu.make_async_copy(
            stages[i], outs[i].at[pl.ds(first, srcs[i].shape[0]), lax.rem(z, 2)], local_sem.at[i, 1]
        )

    def gate(piece, cond):
        return cond if piece[6] is None else jnp.logical_and(cond, tower == piece[6])

    def send_own(k):
        piece = pieces[k]

        @pl.when(gate(piece, place == 0))
        def _():
            move(k, own(piece), slot_of[0], line, 0, 0, {MP: ahead}).start()

        @pl.when(gate(piece, place == 1))
        def _():
            move(k, own(piece), slot_of[1], line, 1, 1, {MP: ahead}).start()
            move(k, own(piece), slot_of[1], line, 2, 1, {MP: behind}).start()

    orders = {t: [k for k, p in enumerate(pieces) if p[6] in (None, t)] for t in (0, 1)}

    def launch(t, place):
        if place >= len(orders[t]):
            return
        k = orders[t][place]

        @pl.when(jnp.logical_and(holder, tower == t))
        def _():
            if far_src and k == far_src[0]:
                twin_copy().wait_recv()
            send_own(k)

    def own_sent(k):
        piece = pieces[k]

        @pl.when(gate(piece, place == 0))
        def _():
            move(k, own(piece), slot_of[0], line, 0, 0, {MP: z}).wait_send()

        @pl.when(gate(piece, place == 1))
        def _():
            move(k, own(piece), slot_of[1], line, 1, 1, {MP: z}).wait_send()
            move(k, own(piece), slot_of[1], line, 2, 1, {MP: z}).wait_send()

    def begin():
        if far_src:

            @pl.when(jnp.logical_and(holder, tower == 0))
            def _():
                twin_copy().start()

        for t in (0, 1):
            for start in range(WINDOW):
                launch(t, start)

    def keeps(i):
        flags = {p[6] for p in pieces if p[0] == i}
        flag = None if len(flags) > 1 else flags.pop()
        return holder if flag is None else jnp.logical_and(holder, tower == flag)

    def begin_local():
        for i in range(len(srcs)):

            @pl.when(keeps(i))
            def _(i=i):
                local_in(i).start()

        for i in range(len(srcs)):

            @pl.when(keeps(i))
            def _(i=i):
                local_in(i).wait()
                local_out(i).start()

    def pass_on(k):
        piece = pieces[k]

        @pl.when(gate(piece, place >= 1))
        def _():
            here = spot(piece, slot_of[0], line)
            move(k, here, slot_of[0], line, 0, 0, {MP: z}).wait_recv()
            move(k, here, slot_of[0], line, 3, 2, {DP: other}).start()

        @pl.when(gate(piece, jnp.logical_and(place >= 1, place <= 2)))
        def _():
            here = spot(piece, slot_of[0], line)
            move(k, here, slot_of[0], line, 0, 0, {MP: ahead}).start()

        @pl.when(gate(piece, place != 1))
        def _():
            here = spot(piece, slot_of[1], line)
            move(k, here, slot_of[1], line, 1, 1, {MP: z}).wait_recv()
            move(k, here, slot_of[1], line, 4, 3, {DP: other}).start()

        @pl.when(gate(piece, place == 2))
        def _():
            here = spot(piece, slot_of[1], line)
            move(k, here, slot_of[1], line, 1, 1, {MP: ahead}).start()

        own_sent(k)
        for t in (0, 1):
            if k in orders[t]:
                launch(t, orders[t].index(k) + WINDOW)

    def arrived(k):
        piece = pieces[k]

        @pl.when(gate(piece, place >= 1))
        def _():
            move(k, spot(piece, slot_of[0], 1 - line), slot_of[0], 1 - line, 3, 2, {DP: dp}).wait_recv()

        @pl.when(gate(piece, place != 1))
        def _():
            move(k, spot(piece, slot_of[1], 1 - line), slot_of[1], 1 - line, 4, 3, {DP: dp}).wait_recv()

    def sent(k):
        piece = pieces[k]

        @pl.when(gate(piece, jnp.logical_or(place == 1, place == 2)))
        def _():
            move(k, spot(piece, slot_of[0], line), slot_of[0], line, 0, 0, {MP: z}).wait_send()

        @pl.when(gate(piece, place == 2))
        def _():
            move(k, spot(piece, slot_of[1], line), slot_of[1], line, 1, 1, {MP: z}).wait_send()

        @pl.when(gate(piece, place >= 1))
        def _():
            move(k, spot(piece, slot_of[0], line), slot_of[0], line, 3, 2, {DP: dp}).wait_send()

        @pl.when(gate(piece, place != 1))
        def _():
            move(k, spot(piece, slot_of[1], line), slot_of[1], line, 4, 3, {DP: dp}).wait_send()

    def end_local(i):
        @pl.when(keeps(i))
        def _():
            local_out(i).wait()

    def end_twin():
        @pl.when(jnp.logical_and(holder, tower == 0))
        def _():
            twin_copy().wait_send()

    return begin, begin_local, pass_on, arrived, sent, end_local, end_twin


def token_steps(blocks, outs, stage, sems):
    send_sem, recv_sem, local_sem = sems
    tower, dp, z, core, line, other, partner = spots()
    stays = z == 3 * core
    size = blocks[0].shape[0]

    def rows(which_core):
        return pl.ds(pl.multiple_of(which_core * size, 16), size)

    def away(i):
        target = {DP: 2 * line + lax.rem(z, 2), MP: 2 * core + z // 2}
        return pltpu.make_async_remote_copy(
            src_ref=blocks[i],
            dst_ref=outs[i].at[rows(lax.rem(z, 2)), :],
            send_sem=send_sem.at[i, 0],
            recv_sem=recv_sem.at[i, 0],
            device_id=target,
            device_id_type=MESH,
        )

    def across(i, which_core):
        return pltpu.make_async_remote_copy(
            src_ref=outs[i].at[rows(which_core), :],
            dst_ref=outs[i].at[rows(which_core), :],
            send_sem=send_sem.at[i, 1],
            recv_sem=recv_sem.at[i, 1],
            device_id={DP: partner},
            device_id_type=MESH,
        )

    def begin(i):
        @pl.when(jnp.logical_not(stays))
        def _():
            away(i).start()

        @pl.when(stays)
        def _():
            first = pltpu.make_async_copy(blocks[i], stage.at[i], local_sem.at[i, 0])
            first.start()
            first.wait()
            second = pltpu.make_async_copy(stage.at[i], outs[i].at[rows(core), :], local_sem.at[i, 1])
            second.start()
            second.wait()
            across(i, core).start()

    def relay(i):
        @pl.when(jnp.logical_not(stays))
        def _():
            away(i).wait_recv()
            across(i, core).start()

    def finish(i):
        across(i, 1 - core).wait_recv()
        across(i, core).wait_send()

        @pl.when(jnp.logical_not(stays))
        def _():
            away(i).wait_send()

    return begin, relay, finish


TILE = 32
LAG = 1
WINDOW = 2


def barrier_all(peers, options):
    for cond, target in peers:
        if cond is None:
            greet(target)
        else:
            pl.when(cond)(functools.partial(greet, target))
    for cond, count in options:

        @pl.when(cond)
        def _(count=count):
            pl.semaphore_wait(pltpu.get_barrier_semaphore(), count)


def fold_rows(tile):
    return jnp.sum(tile.reshape(tile.shape[0] // 8, 8, tile.shape[1]), axis=0)


def row_tiles(total, run, carry, first=0, unroll=1):
    tile = next(t for t, by in ((64, 192), (96, 96), (48, 48), (32, 32)) if total % by == 0)
    turns = total // tile

    def step(i, kept):
        return run(pl.ds(pl.multiple_of(first + i * tile, 16), tile), kept)

    return lax.fori_loop(0, turns, step, carry, unroll=unroll)


def norm_back_tile(values, gain, grads):
    unit, scale = norm_parts(values)
    inner = grads * gain
    mean_one = jnp.mean(inner, axis=-1, keepdims=True)
    mean_two = jnp.mean(inner * unit, axis=-1, keepdims=True)
    return ((inner - mean_one - unit * mean_two) * scale, fold_rows(grads * unit), fold_rows(grads))


def gelu_both(v):
    rate = 0.7978845608028654
    square = v * v
    bend = jnp.tanh(rate * (v + 0.044715 * (square * v)))
    lifted = 0.5 * (1.0 + bend)
    slope = lifted + 0.5 * v * (1.0 - bend * bend) * (rate * (1.0 + 3.0 * 0.044715 * square))
    return (v * lifted, slope)


def low_lanes_of(count):
    return lax.broadcasted_iota(jnp.int32, (count, LANES), 1) < HDIM


def stack_all(block, low):
    wide = block.astype(F32)
    return jnp.concatenate([jnp.where(low, wide, 0.0), jnp.where(low, 0.0, wide)], axis=0)


def merge_all(both, low):
    count = both.shape[0] // 2
    return jnp.where(low, both[:count], both[count:])


def lane_block(index):
    return pl.ds(pl.multiple_of(index * LANES, LANES), LANES)


def scores_of(keys, queries, mask):
    scores = dot_rows(keys, queries)
    if mask is None:
        return scores
    block = mask[...]
    return scores + jnp.concatenate([block, block], axis=1)


def forward_heads(queries, keys, vals, mask, low):
    scores = scores_of(keys, queries, mask)
    top = jnp.max(scores, axis=0, keepdims=True)
    grown = jnp.exp(scores - top)
    total = jnp.sum(grown, axis=0, keepdims=True)
    weights = (grown * (1.0 / total)).astype(BF16)
    return (merge_all(dot_first(weights, vals), low), top + jnp.log(total))


def backward_heads(queries, keys, vals, grads, tops, mask, low, scale):
    weights = jnp.exp(scores_of(keys, queries, mask) - tops)
    grad_w = dot_rows(vals, grads)
    row_dot = jnp.sum(weights * grad_w, axis=0, keepdims=True)
    grad_s = (weights * (grad_w - row_dot)).astype(BF16)
    grad_q = merge_all(dot_first(keys, grad_s).T, low) * scale
    return (grad_q, dot_plain(grad_s, queries), dot_plain(weights.astype(BF16), grads))


def fill_mask(mask, col, row, is_dec):
    count = mask.shape[0]

    def tile(rows, kept):
        shape = (rows.size, count)
        key_at = lax.broadcasted_iota(jnp.int32, shape, 0) + rows.start
        query_at = lax.broadcasted_iota(jnp.int32, shape, 1)
        allowed = jnp.logical_and(key_at <= query_at, col[rows, 0:1] == row[0:1, :])
        mask[rows, :] = jnp.where(jnp.logical_or(allowed, jnp.logical_not(is_dec)), 0.0, NEG)
        return kept

    row_tiles(count, tile, 0)


def self_forward(packed, mask, out, tops, pairs, scale):
    low = low_lanes_of(packed.shape[0])

    @pl.loop(0, pairs)
    def _(pair):
        queries = (stack_all(packed[:, lane_block(pair)], low) * scale).astype(BF16)
        mixed, top = forward_heads(
            queries, packed[:, lane_block(pairs + pair)], packed[:, lane_block(2 * pairs + pair)], mask, low
        )
        out[:, lane_block(pair)] = mixed.astype(BF16)
        tops[pair, 0:1, :] = top


def self_backward(packed, grads, tops, mask, out, pairs, scale, between):
    low = low_lanes_of(packed.shape[0])

    @pl.loop(0, pairs)
    def _(pair):
        queries = (stack_all(packed[:, lane_block(pair)], low) * scale).astype(BF16)
        head_grads = stack_all(grads[:, lane_block(pair)], low).astype(BF16)
        grad_q, grad_k, grad_v = backward_heads(
            queries,
            packed[:, lane_block(pairs + pair)],
            packed[:, lane_block(2 * pairs + pair)],
            head_grads,
            tops[pair, 0:1, :],
            mask,
            low,
            scale,
        )
        out[:, lane_block(pair)] = grad_q.astype(BF16)
        out[:, lane_block(pairs + pair)] = grad_k.astype(BF16)
        out[:, lane_block(2 * pairs + pair)] = grad_v.astype(BF16)
        pl.when(pair == 1)(between)


def cross_forward(image, query, keys, vals, picks, out, tops, pairs, scale):
    low = low_lanes_of(query.shape[0])

    @pl.loop(0, pairs)
    def _(pair):
        cols = lane_block(pair)
        queries = (stack_all(query[:, cols], low) * scale).astype(BF16)
        mixed, top = forward_heads(queries, keys[image, :, cols], vals[image, :, cols], None, low)
        kept = jnp.where(picks[...] == image, mixed, out[:, cols].astype(F32))
        out[:, cols] = kept.astype(BF16)
        tops[image, pair, 0:1, :] = top


def cross_backward(query, keys, vals, grads, picks, tops, dq, dk, dv, sum_q, pairs, scale):
    low = low_lanes_of(query.shape[0])

    @pl.loop(0, pairs)
    def _(pair):
        cols = lane_block(pair)
        queries = (stack_all(query[:, cols], low) * scale).astype(BF16)
        sum_q[...] = jnp.zeros_like(sum_q)

        @pl.loop(0, 2)
        def _(image):
            own = jnp.where(picks[...] == image, grads[:, cols].astype(F32), 0.0)
            grad_q, grad_k, grad_v = backward_heads(
                queries,
                keys[image, :, cols],
                vals[image, :, cols],
                stack_all(own, low).astype(BF16),
                tops[image, pair, 0:1, :],
                None,
                low,
                scale,
            )
            sum_q[...] += grad_q
            dk[image, :, cols] = grad_k.astype(BF16)
            dv[image, :, cols] = grad_v.astype(BF16)

        dq[:, cols] = sum_q[...].astype(BF16)


class Reducer:
    def __init__(self, grads, near, far, outs, sems, window, first, last):
        self.grads, self.near, self.far, self.outs = grads, near, far, outs
        self.y_send, self.y_recv, self.z_send, self.z_recv, self.c_send, self.c_recv = sems
        self.tower, self.dp, self.z, self.core, self.line, self.other, self.partner = spots()
        self.place = self.z + self.core * (3 - 2 * self.z)
        self.holder = self.place <= 1
        self.slot = lax.rem(self.z, 2)
        self.half = grads.shape[3] // 2
        self.rows = grads.shape[2]
        self.window, self.first, self.last = window, first, last

    def lanes(self, line):
        return pl.ds(pl.multiple_of(line * self.half, LANES), self.half)

    def to_line(self, k):
        return pltpu.make_async_remote_copy(
            src_ref=self.grads.at[k, :, :, self.lanes(1 - self.line)],
            dst_ref=self.near.at[k],
            send_sem=self.y_send.at[k],
            recv_sem=self.y_recv.at[k],
            device_id={DP: self.other},
            device_id_type=MESH,
        )

    def send(self, source, target, k, sent, got, where):
        return pltpu.make_async_remote_copy(
            src_ref=source,
            dst_ref=target,
            send_sem=self.z_send.at[k, sent],
            recv_sem=self.z_recv.at[k, got],
            device_id={MP: where},
            device_id_type=MESH,
        )

    def inward(self, k):
        return self.send(self.near.at[k], self.far.at[k], k, 0, 0, 2 - self.core)

    def beside(self, k):
        return self.send(self.near.at[k, 1 - self.slot], self.far.at[k, 0], k, 0, 0, 4 * self.core + 1 - self.z)

    def onward(self, k, shard):
        return self.send(self.near.at[k, shard], self.far.at[k, 1], k, shard, 1, 2 * self.core + shard)

    def to_core(self, k):
        return pltpu.make_async_remote_copy(
            src_ref=self.outs.at[k],
            dst_ref=self.outs.at[k],
            send_sem=self.c_send.at[k],
            recv_sem=self.c_recv.at[k],
            device_id={DP: self.partner},
            device_id_type=MESH,
        )

    def launch(self, k):
        self.to_line(k).start()

    def tiles(self, run):
        @pl.loop(0, self.rows // TILE)
        def _(i):
            run(pl.ds(pl.multiple_of(i * TILE, TILE), TILE))

    def add_near(self, k, more=True):
        self.to_line(k).wait_send()
        self.to_line(k).wait_recv()
        if more:
            pl.when(k + self.window < self.last)(lambda: self.launch(k + self.window))

        def run(rows):
            for b in range(2):
                total = self.grads[k, b, rows, self.lanes(self.line)].astype(F32) + self.near[k, b, rows, :].astype(F32)
                self.near[k, b, rows, :] = total.astype(BF16)

        self.tiles(run)
        pl.when(self.place == 3)(self.inward(k).start)
        pl.when(self.holder)(self.beside(k).start)

    def add_mid(self, k):
        @pl.when(self.place == 2)
        def _():
            self.inward(k).wait_recv()

            def run(rows):
                for b in range(2):
                    total = self.near[k, b, rows, :].astype(F32) + self.far[k, b, rows, :].astype(F32)
                    self.near[k, b, rows, :] = total.astype(BF16)

            self.tiles(run)
            for shard in range(2):
                self.onward(k, shard).start()

    def add_far(self, k):
        @pl.when(self.holder)
        def _():
            self.beside(k).wait_recv()
            self.onward(k, 0).wait_recv()

            def run(rows):
                total = self.near[k, self.slot, rows, :].astype(F32)
                for seat in range(2):
                    total = total + self.far[k, seat, rows, :].astype(F32)
                self.outs[k, rows, :] = total.astype(BF16)

            self.tiles(run)
            self.to_core(k).start()

    def step(self, k):
        self.add_near(k)
        pl.when(k - LAG >= self.first)(lambda: self.add_mid(k - LAG))

    def drain(self, begin):
        @pl.loop(begin, self.last + 2 * LAG)
        def _(i):
            pl.when(i < self.last)(lambda: self.add_near(i))
            j = i - LAG
            pl.when(jnp.logical_and(j >= self.first, j < self.last))(lambda: self.add_mid(j))
            n = j - LAG
            pl.when(jnp.logical_and(n >= begin - 2 * LAG, n >= self.first))(lambda: self.add_far(n))

    def far_before(self, begin):
        @pl.loop(self.first, jnp.maximum(self.first, begin - 2 * LAG))
        def _(k):
            self.add_far(k)

    def close(self):
        @pl.loop(self.first, self.last)
        def _(k):
            pl.when(self.place == 3)(self.inward(k).wait_send)

            @pl.when(self.place == 2)
            def _():
                for shard in range(2):
                    self.onward(k, shard).wait_send()

            @pl.when(self.holder)
            def _():
                self.beside(k).wait_send()
                self.to_core(k).wait_send()

            @pl.when(jnp.logical_not(self.holder))
            def _():
                self.to_core(k).wait_recv()


class Tail(NamedTuple):
    d_three: Any
    base: Any
    upstream: Any
    gains: Any
    smalls: Any
    hid: Any
    w_mlp: Any
    pre: Any
    act: Any
    w_in: Any
    x1: Any
    w_out: Any
    mixed: Any
    packed: Any
    tops: Any
    seg_col: Any
    seg_row: Any
    a_one: Any
    w_qkv: Any
    x0: Any


IMAGE_ONLY = Tail._fields[5:11]


def tail_kernel(pairs, scale, *refs):
    it = iter(refs)
    hbm = Tail(*[next(it) for _ in Tail._fields])
    cross_in = next(it)
    outs = next(it)
    small_out, grad_out, from_text = next(it), next(it), next(it)
    vm = Tail(*[next(it) for _ in Tail._fields])
    grads, near, far = next(it), next(it), next(it)
    g_f32, g_low, grad_hid, grad_pre, d_packed, mix_grad = (next(it) for _ in range(6))
    part_send, part_recv, mask, smalls, small_near, small_all, own_grad = (next(it) for _ in range(7))
    load_sem, red_sems, part_sem, small_sem, move_sem, twin_sem = next(it), [next(it) for _ in range(6)], next(it), next(it), next(it), next(it)
    tower, dp, z, core, line, other, partner = spots()
    is_enc = tower == 0
    is_dec = tower == 1
    stays = z == 3 * core
    tokens, width = g_f32.shape
    rows_txt = tokens // LTXT
    quarter = tokens // 2
    heads = mix_grad.shape[1]
    rows_of = grads.shape[2]
    ffn_blocks = width // rows_of

    home = {DP: 2 * line + z // 2, MP: 2 * lax.rem(z, 2) + core}
    guest = {DP: 2 * line + lax.rem(z, 2), MP: 2 * core + z // 2}
    moved = jnp.logical_not(stays)
    peers = [(None, {DP: other}), (None, {DP: partner}), (is_enc, {TOWER: 1 - tower})]
    peers += [(None, {MP: lax.rem(z + away, 4)}) for away in range(1, 4)]
    peers += [(moved, home), (moved, guest)]
    barrier_all(
        peers,
        [
            (jnp.logical_and(is_enc, stays), 5),
            (jnp.logical_and(is_enc, moved), 7),
            (jnp.logical_and(is_dec, stays), 6),
            (jnp.logical_and(is_dec, moved), 8),
        ],
    )

    def load(i):
        return pltpu.make_async_copy(hbm[i], vm[i], load_sem.at[i])

    def on_side(i, run):
        if Tail._fields[i] in IMAGE_ONLY:
            pl.when(is_enc)(run)
        else:
            run()

    pl.when(is_dec)(lambda: pltpu.make_async_copy(cross_in, grads.at[pl.ds(ffn_blocks, ffn_blocks)], load_sem.at[len(hbm)]).start())
    for i in range(len(hbm)):
        on_side(i, load(i).start)

    def need(*wanted):
        for i, ref in enumerate(vm):
            if any(ref is one for one in wanted):
                on_side(i, load(i).wait)

    first_block = ffn_blocks * tower
    blocks = grads.shape[0]
    red = Reducer(grads, near, far, outs, red_sems, 2, first_block, blocks)

    def twin_copy():
        return pltpu.make_async_remote_copy(
            src_ref=outs.at[pl.ds(ffn_blocks, 2)],
            dst_ref=from_text,
            send_sem=twin_sem.at[0],
            recv_sem=twin_sem.at[1],
            device_id={TOWER: 1 - tower},
            device_id_type=MESH,
        )

    cross_load = pltpu.make_async_copy(cross_in, grads.at[pl.ds(ffn_blocks, ffn_blocks)], load_sem.at[len(hbm)])

    @pl.when(is_dec)
    def _():
        cross_load.wait()
        red.launch(ffn_blocks)

    def home_move(source, target, k):
        return pltpu.make_async_remote_copy(
            src_ref=source,
            dst_ref=target,
            send_sem=move_sem.at[k, 0],
            recv_sem=move_sem.at[k, 1],
            device_id=home,
            device_id_type=MESH,
        )

    def part_copy(k):
        return pltpu.make_async_remote_copy(
            src_ref=part_send.at[k],
            dst_ref=part_recv.at[k],
            send_sem=part_sem.at[k, 0],
            recv_sem=part_sem.at[k, 1],
            device_id={DP: partner},
            device_id_type=MESH,
        )

    zero = jnp.zeros((8, width), F32)
    need(vm.d_three, vm.base, vm.upstream, vm.gains, vm.smalls)
    smalls[...] = vm.smalls[...]

    def put(row, value):
        smalls[pl.ds(row, 1), :] = jnp.sum(value, axis=0, keepdims=True)

    def third(rows, kept):
        back, dg, db = norm_back_tile(vm.base[rows, :], vm.gains[2], vm.d_three[rows, :])
        total = vm.upstream[rows, :] + back
        g_f32[rows, :] = total
        low = total.astype(BF16)
        g_low[rows, :] = low
        return (kept[0] + dg, kept[1] + db, kept[2] + fold_rows(low.astype(F32)))

    dg, db, bias = row_tiles(tokens, third, (zero, zero, zero), 0, 3)
    put(4, dg)
    put(7, db)

    @pl.when(is_enc)
    def _():
        put(1, bias)
        need(vm.hid)

        @pl.loop(0, 2)
        def _(b):
            made = dot_first(vm.hid[:, pl.ds(pl.multiple_of(b * width, LANES), width)], g_low[...]).astype(BF16)
            grads[0:ffn_blocks, b] = made.reshape(ffn_blocks, rows_of, width)

        red.launch(0)
        need(vm.w_mlp, vm.pre)

        @pl.loop(0, 2)
        def _(b):
            cols = pl.ds(pl.multiple_of(b * width, LANES), width)
            grad_hid[...] = dot_rows(g_low[...], vm.w_mlp[cols, :])

            def bend(rows, kept):
                low = (grad_hid[rows, :] * gelu_both(vm.pre[rows, cols])[1]).astype(BF16)
                grad_pre[b, rows, :] = low
                return kept + fold_rows(low.astype(F32))

            put(9 + b, row_tiles(tokens, bend, zero))

        red.launch(1)
        need(vm.act, vm.w_in)

        @pl.loop(0, 2)
        def _(b):
            made = dot_first(grad_pre[b], vm.act[...]).astype(BF16)
            grads[ffn_blocks : 2 * ffn_blocks, b] = made.reshape(ffn_blocks, rows_of, width)

        red.step(0)
        grad_hid[...] = jnp.zeros_like(grad_hid)

        @pl.loop(0, 2)
        def _(b):
            grad_hid[...] += dot_rows(grad_pre[b], vm.w_in[b])

        def lower(rows, kept):
            part_send[0, rows, :] = grad_hid[rows, :].astype(BF16)
            return kept

        row_tiles(tokens, lower, 0)
        part_copy(0).start()
        need(vm.x1)
        part_copy(0).wait()

        def second(rows, kept):
            grad = part_send[0, rows, :].astype(F32) + part_recv[0, rows, :].astype(F32)
            back, dg, db = norm_back_tile(vm.x1[rows, :], vm.gains[1], grad)
            total = g_f32[rows, :] + back
            g_f32[rows, :] = total
            low = total.astype(BF16)
            g_low[rows, :] = low
            return (kept[0] + dg, kept[1] + db, kept[2] + fold_rows(low.astype(F32)))

        dg, db, bias_two = row_tiles(tokens, second, (zero, zero, zero), 0, 3)
        put(3, dg)
        put(6, db)
        put(0, bias_two)
        red.step(1)

    @pl.when(is_dec)
    def _():
        put(0, bias)
        red.launch(ffn_blocks + 1)

    need(vm.w_out, vm.mixed, vm.packed, vm.tops, vm.seg_col, vm.seg_row)
    mix_grad[...] = dot_rows(g_low[...], vm.w_out[...]).astype(BF16)
    grads[2 * ffn_blocks] = dot_first(vm.mixed[...], g_low[...]).astype(BF16).reshape(grads.shape[1:])
    now = 2 + (ffn_blocks - 2) * tower

    fill_mask(mask, vm.seg_col, vm.seg_row, is_dec)
    red.step(now)
    self_backward(vm.packed, mix_grad, vm.tops, mask, d_packed, pairs, scale, lambda: red.step(now + 1))
    red.step(now + 2)


    need(vm.a_one, vm.w_qkv, vm.x0)
    grad_hid[...] = jnp.zeros_like(grad_hid)

    @pl.loop(0, 3)
    def _(a):
        cols = pl.ds(pl.multiple_of(a * heads, LANES), heads)
        made = dot_first(d_packed[:, cols], vm.a_one[...]).astype(BF16)
        grads[2 * ffn_blocks + 1 + a] = made.reshape(grads.shape[1:])
        grad_hid[...] += dot_plain(d_packed[:, cols], vm.w_qkv[cols, :])

    red.step(now + 3)


    def lower_two(rows, kept):
        part_send[1, rows, :] = grad_hid[rows, :].astype(BF16)
        return (
            kept[0] + fold_rows(d_packed[rows, pl.ds(0, heads)].astype(F32)),
            kept[1] + fold_rows(d_packed[rows, pl.ds(2 * heads, heads)].astype(F32)),
        )

    small_zero = jnp.zeros((8, heads), F32)
    q_sum, v_sum = row_tiles(tokens, lower_two, (small_zero, small_zero))
    part_copy(1).start()
    smalls[8:9, :] = jnp.concatenate(
        [jnp.sum(q_sum, axis=0, keepdims=True), jnp.sum(v_sum, axis=0, keepdims=True)], axis=1
    )
    part_copy(1).wait()

    def first(rows, kept):
        grad = part_send[1, rows, :].astype(F32) + part_recv[1, rows, :].astype(F32)
        back, dg, db = norm_back_tile(vm.x0[rows, :].astype(F32), vm.gains[0], grad)
        part_send[1, rows, :] = (g_f32[rows, :] + back).astype(BF16)
        return (kept[0] + dg, kept[1] + db)

    dg, db = row_tiles(tokens, first, (zero, zero), 0, 3)
    put(2, dg)
    put(5, db)
    mine = pl.ds(pl.multiple_of(core * quarter, TILE), quarter)

    def own_copy(rows, kept):
        shifted = pl.ds(pl.multiple_of(core * quarter + rows.start, 32), rows.size)
        own_grad[rows, :] = part_send[1, shifted, :]
        return kept

    row_tiles(quarter, own_copy, 0)
    red.step(now + 4)

    small_line = pltpu.make_async_remote_copy(
        src_ref=smalls,
        dst_ref=small_near,
        send_sem=small_sem.at[0],
        recv_sem=small_sem.at[1],
        device_id={DP: other},
        device_id_type=MESH,
    )
    small_line.start()

    @pl.when(moved)
    def _():
        home_move(own_grad, grad_out, 1).start()

    @pl.when(stays)
    def _():
        pltpu.make_async_copy(own_grad, grad_out, move_sem.at[1, 0]).start()


    def small_pair(sender, away):
        return pltpu.make_async_remote_copy(
            src_ref=small_all.at[sender],
            dst_ref=small_all.at[sender],
            send_sem=small_sem.at[1 + away],
            recv_sem=small_sem.at[4 + away],
            device_id={MP: lax.rem(z + away, 4)},
            device_id_type=MESH,
        )

    def small_core(which):
        return pltpu.make_async_remote_copy(
            src_ref=small_out.at[which],
            dst_ref=small_out.at[which],
            send_sem=small_sem.at[8],
            recv_sem=small_sem.at[9],
            device_id={DP: partner},
            device_id_type=MESH,
        )

    small_line.wait()
    small_all[z] = smalls[...] + small_near[...]


    for away in range(1, 4):
        small_pair(z, away).start()

    red.far_before(now + 5)
    red.drain(now + 5)
    red.close()
    pl.when(is_dec)(twin_copy().start)

    for away in range(1, 4):
        small_pair(lax.rem(z + 4 - away, 4), away).wait_recv()
    small_out[core] = ((small_all[0] + small_all[1]) + small_all[2]) + small_all[3]
    small_core(core).start()
    for away in range(1, 4):
        small_pair(z, away).wait_send()

    @pl.when(moved)
    def _():
        home_move(own_grad, grad_out, 1).wait()

    @pl.when(stays)
    def _():
        pltpu.make_async_copy(own_grad, grad_out, move_sem.at[1, 0]).wait()

    pl.when(is_dec)(twin_copy().wait_send)
    pl.when(is_enc)(twin_copy().wait_recv)
    small_core(core).wait_send()
    small_core(1 - core).wait_recv()


def tail(values, cross_grad, scale):
    tokens, width = values.base.shape
    heads = values.mixed.shape[1]
    pairs = heads // LANES
    hidden = values.pre.shape[1]
    quarter = tokens // 2
    half = width // 2
    rows_of = heads // 2
    blocks = 2 * (width // rows_of) + 4
    assert hidden == 2 * width and cross_grad.shape[0] == width // rows_of
    hbm = pl.BlockSpec(memory_space=pltpu.HBM)
    vmem = pl.BlockSpec(memory_space=pltpu.VMEM)
    n_in = len(values)
    scratch = [pltpu.VMEM(x.shape, x.dtype) for x in values]
    scratch += [pltpu.VMEM((blocks, 2, rows_of, width), BF16)]
    scratch += [pltpu.VMEM((blocks, 2, rows_of, half), BF16)] * 2
    scratch += [
        pltpu.VMEM((tokens, width), F32),
        pltpu.VMEM((tokens, width), BF16),
        pltpu.VMEM((tokens, width), F32),
        pltpu.VMEM((2, tokens, hidden // 2), BF16),
        pltpu.VMEM((tokens, 3 * heads), BF16),
        pltpu.VMEM((tokens, heads), BF16),
        pltpu.VMEM((2, tokens, width), BF16),
        pltpu.VMEM((2, tokens, width), BF16),
        pltpu.VMEM((tokens, tokens), F32),
        pltpu.VMEM(values.smalls.shape, F32),
        pltpu.VMEM(values.smalls.shape, F32),
        pltpu.VMEM((4,) + values.smalls.shape, F32),
        pltpu.VMEM((quarter, width), BF16),
    ]
    dma = pltpu.SemaphoreType.DMA
    scratch += [dma((n_in + 1,)), dma((blocks,)), dma((blocks,)), dma((blocks, 2)), dma((blocks, 2)), dma((blocks,)), dma((blocks,))]
    scratch += [dma((2, 2)), dma((10,)), dma((2, 2)), dma((2,))]
    out_shape = [jax.ShapeDtypeStruct((blocks, rows_of, half), BF16)]
    out_shape += [
        jax.ShapeDtypeStruct((2,) + values.smalls.shape, F32),
        jax.ShapeDtypeStruct((quarter, width), BF16),
        jax.ShapeDtypeStruct((2, heads // 2, half), BF16),
    ]
    return pl.pallas_call(
        functools.partial(tail_kernel, pairs, scale),
        in_specs=[hbm] * (n_in + 1),
        out_specs=[vmem] * 2 + [hbm] * 2,
        out_shape=out_shape,
        scratch_shapes=scratch,
        compiler_params=pltpu.CompilerParams(
            collective_id=1, has_side_effects=True, vmem_limit_bytes=TAIL_LIMIT
        ),
        name="tail",
    )(*values, cross_grad)


class Head(NamedTuple):
    packed: Any
    mixed: Any
    tops: Any
    a_one: Any
    x1: Any
    base: Any
    act_three: Any
    act: Any
    pre: Any
    hid: Any
    query: Any


def head_kernel(pieces, pairs, scale, *refs):
    it = iter(refs)
    srcs = [next(it) for _ in range(5)]
    blocks = [next(it)]
    seg_ref, image_ref = next(it), next(it)
    gains, shifts, out_b, ffn_out_b, ffn_in_b, qv_b = (next(it) for _ in range(6))
    outs = [next(it) for _ in range(5)]
    tokens = [next(it)]
    seg_out = [next(it) for _ in range(3)]
    hbm = Head(*[next(it) for _ in Head._fields])
    stages = [next(it) for _ in range(5)]
    weight_sems = [next(it) for _ in range(5)]
    token_stage = next(it)
    token_sems = [next(it) for _ in range(3)]
    w_qkv, w_out, w_q, w_in, w_mlp = (next(it) for _ in range(5))
    vm = Head(*[next(it) for _ in Head._fields])
    part_send, part_recv, raw, mask = next(it), next(it), next(it), next(it)
    seg_sem, load_sem, store_sem, part_sem = (next(it) for _ in range(4))
    tower, dp, z, core, line, other, partner = spots()
    is_enc = tower == 0
    is_dec = tower == 1
    stays = z == 3 * core
    moved = jnp.logical_not(stays)
    count, width = vm.x1.shape
    rows_txt = count // LTXT
    heads = vm.mixed.shape[1]
    at_end = jnp.logical_or(z == 0, z == 3)

    peers = [(z > 0, {MP: z - 1}), (z < 3, {MP: z + 1})]
    peers += [(None, {DP: other}), (None, {TOWER: 1 - tower}), (None, {DP: partner})]
    peers += [
        (moved, {DP: 2 * line + lax.rem(z, 2), MP: 2 * core + z // 2}),
        (moved, {DP: 2 * line + z // 2, MP: 2 * lax.rem(z, 2) + core}),
    ]
    barrier_all(
        peers,
        [(stays, 4), (jnp.logical_and(at_end, moved), 6), (jnp.logical_not(at_end), 7)],
    )

    begin, begin_local, pass_on, arrived, sent, end_local, end_twin = weight_steps(
        pieces, srcs, outs, stages, weight_sems
    )
    token_begin, token_relay, token_finish = token_steps(blocks, tokens, token_stage, token_sems)
    token_begin(0)
    begin()

    has_notes = core == z // 2

    def note_send(i):
        return pltpu.make_async_remote_copy(
            src_ref=seg_out[i],
            dst_ref=seg_out[i],
            send_sem=seg_sem.at[i, 0],
            recv_sem=seg_sem.at[i, 1],
            device_id={DP: partner},
            device_id_type=MESH,
        )

    @pl.when(has_notes)
    def _():
        rows = seg_ref.shape[0] // 2
        side = lax.rem(z, 2)
        segs = jnp.where(side == 0, seg_ref[0:rows, :], seg_ref[rows : 2 * rows, :])
        marks = segs + LTXT * lax.broadcasted_iota(jnp.int32, segs.shape, 0)
        tall = jnp.concatenate([marks.astype(F32), jnp.zeros((16 - rows, LTXT), F32)], axis=0).T
        seg_out[1][...] = jnp.zeros_like(seg_out[1])
        for r in range(rows):
            at = pl.ds(r * LTXT, LTXT)
            seg_out[0][at, :] = jnp.broadcast_to(tall[:, r : r + 1], (LTXT, LANES)).astype(jnp.int32)
            seg_out[1][0:1, at] = marks[r : r + 1, :]
            seg_out[2][at, :] = jnp.full((LTXT, LANES), image_ref[side * rows + r], jnp.int32)
        for i in range(3):
            note_send(i).start()

    begin_local()
    token_relay(0)

    def load(i, target, source):
        return pltpu.make_async_copy(source, target, load_sem.at[i])

    def store(ref):
        i = [x is ref for x in vm].index(True)
        return pltpu.make_async_copy(vm[i], hbm[i], store_sem.at[i])

    def part_copy(k):
        return pltpu.make_async_remote_copy(
            src_ref=part_send.at[k],
            dst_ref=part_recv.at[k],
            send_sem=part_sem.at[k, 0],
            recv_sem=part_sem.at[k, 1],
            device_id={DP: partner},
            device_id_type=MESH,
        )

    def normed(source, target, which):
        gain, shift = gains[which], shifts[which]

        def tile(rows, kept):
            unit, _ = norm_parts(source[rows, :].astype(F32))
            target[rows, :] = (unit * gain + shift).astype(BF16)
            return kept

        row_tiles(count, tile, 0, 0, 3)

    def chosen(which, flag, far=False):
        return [k for k, p in enumerate(pieces) if p[0] == which and p[6] == flag and p[7] == far]

    enc_in, enc_mlp, dec_in = chosen(3, 0), chosen(4, 0), chosen(3, 1) + chosen(4, 1)
    k_qkv, k_out, k_own, k_far = chosen(0, None), chosen(1, None), chosen(2, 1), chosen(2, 1, True)
    waiting = {0: enc_in + enc_mlp, 1: k_own + k_far + dec_in}

    def relay(enc=0, dec=0):
        for t, count in ((0, enc), (1, dec)):
            for k in waiting[t][:count]:
                pass_on(k)
            waiting[t] = waiting[t][count:]

    token_finish(0)
    normed(tokens[0], vm.a_one, 0)
    store(vm.a_one).start()
    for k in k_qkv + k_out:
        pass_on(k)
    for k in k_qkv:
        arrived(k)
    end_local(0)
    load(0, w_qkv, outs[0]).start()
    load(0, w_qkv, outs[0]).wait()

    @pl.loop(0, 3)
    def _(part):
        cols = pl.ds(pl.multiple_of(part * heads, LANES), heads)
        own = pl.ds(pl.multiple_of(core * heads, LANES), heads)
        bias = jnp.where(part == 1, 0.0, qv_b[pl.ds(part // 2, 1), own])
        made = dot_rows(vm.a_one[...], w_qkv[part].reshape(heads, width)) + bias
        vm.packed[:, cols] = made.astype(BF16)

    store(vm.packed).start()

    @pl.when(has_notes)
    def _():
        for i in range(3):
            note_send(i).wait_send()

    @pl.when(jnp.logical_not(has_notes))
    def _():
        for i in range(3):
            note_send(i).wait_recv()

    relay(1, 1)
    fill_mask(mask, seg_out[0], seg_out[1], is_dec)
    self_forward(vm.packed, mask, vm.mixed, vm.tops, pairs, scale)
    store(vm.mixed).start()
    store(vm.tops).start()
    for k in k_out:
        arrived(k)
    end_local(1)
    load(1, w_out, outs[1]).start()
    relay(1, 1)
    load(1, w_out, outs[1]).wait()
    part_send[0] = dot_plain(vm.mixed[...], w_out[0].reshape(heads, width)).astype(BF16)
    part_copy(0).start()
    relay(1, 1)
    part_copy(0).wait()

    def add_one(rows, kept):
        total = part_send[0, rows, :].astype(F32) + part_recv[0, rows, :].astype(F32)
        vm.x1[rows, :] = tokens[0][rows, :].astype(F32) + total + out_b[...]
        return kept

    row_tiles(count, add_one, 0)
    store(vm.x1).start()

    @pl.when(is_enc)
    def _():
        relay(1)
        normed(vm.x1, vm.act, 1)
        store(vm.act).start()
        relay(1)
        for k in enc_in:
            arrived(k)
        end_local(3)
        load(3, w_in, outs[3]).start()
        load(3, w_in, outs[3]).wait()
        relay(1)

        @pl.loop(0, 2)
        def _(b):
            cols = pl.ds(pl.multiple_of(b * width, LANES), width)
            raw[...] = dot_plain(vm.act[...], w_in[0, b])
            bias = ffn_in_b[0:1, pl.ds(pl.multiple_of((2 * core + b) * width, LANES), width)]

            def bend(rows, kept):
                pre = raw[rows, :] + bias
                vm.pre[rows, cols] = pre
                vm.hid[rows, cols] = gelu_tanh(pre).astype(BF16)
                return kept

            row_tiles(count, bend, 0)

        relay(1)
        store(vm.pre).start()
        store(vm.hid).start()
        relay(len(waiting[0]))
        for k in enc_mlp:
            arrived(k)
        end_local(4)
        load(4, w_mlp, outs[4]).start()
        load(4, w_mlp, outs[4]).wait()
        part_send[1] = dot_plain(vm.hid[...], w_mlp[0].reshape(2 * width, width)).astype(BF16)
        part_copy(1).start()
        part_copy(1).wait()

        def add_two(rows, kept):
            total = part_send[1, rows, :].astype(F32) + part_recv[1, rows, :].astype(F32)
            vm.base[rows, :] = vm.x1[rows, :] + total + ffn_out_b[...]
            return kept

        row_tiles(count, add_two, 0)

    @pl.when(is_dec)
    def _():
        def same(rows, kept):
            vm.base[rows, :] = vm.x1[rows, :]
            return kept

        row_tiles(count, same, 0)

    store(vm.base).start()
    normed(vm.base, vm.act_three, 2)
    store(vm.act_three).start()

    @pl.when(is_dec)
    def _():
        relay(0, 2)
        for k in k_own:
            arrived(k)
        end_local(2)
        load(2, w_q, outs[2].at[2]).start()
        load(2, w_q, outs[2].at[2]).wait()
        vm.query[...] = dot_rows(vm.act_three[...], w_q[...].reshape(heads, width)).astype(BF16)
        store(vm.query).start()
        relay(0, len(waiting[1]))
        for k in k_far + dec_in:
            arrived(k)
        end_local(3)
        end_local(4)

    for k in range(len(pieces)):
        sent(k)
    end_twin()
    for ref in vm:
        if ref is vm.act or ref is vm.pre or ref is vm.hid:
            pl.when(is_enc)(store(ref).wait)
        elif ref is vm.query:
            pl.when(is_dec)(store(ref).wait)
        else:
            store(ref).wait()


def head(shards, blocks, segment_ids, row_image, vecs, scale):
    qkv, out, cross, ffn_in, ffn_out = shards
    heads = 2 * out.shape[1]
    width = out.shape[2]
    pairs = heads // LANES
    count = 2 * blocks[0].shape[0]
    hidden = 2 * ffn_in.shape[2]

    def cuts(i, flag):
        blocks_of, rows, _ = shards[i].shape
        cut = rows if rows <= 192 else rows // 4
        return [(i, a, a, 1, at, cut, flag, False) for a in range(blocks_of) for at in range(0, rows, cut)]

    pieces = cuts(0, None) + cuts(1, None)
    rows = cross.shape[1]
    pieces += [(2, 2 + a, a, 1, 0, rows, 1, False) for a in range(2)] + [(2, a, a, 1, 0, rows, 1, True) for a in range(2)]
    pieces += cuts(3, 0) + cuts(4, 0) + cuts(3, 1) + cuts(4, 1)[:2]
    n = len(pieces)
    hbm = pl.BlockSpec(memory_space=pltpu.HBM)
    vmem = pl.BlockSpec(memory_space=pltpu.VMEM)
    struct = jax.ShapeDtypeStruct
    made = Head(
        packed=struct((count, 3 * heads), BF16),
        mixed=struct((count, heads), BF16),
        tops=struct((pairs, 8, 2 * count), F32),
        a_one=struct((count, width), BF16),
        x1=struct((count, width), F32),
        base=struct((count, width), F32),
        act_three=struct((count, width), BF16),
        act=struct((count, width), BF16),
        pre=struct((count, hidden), F32),
        hid=struct((count, hidden), BF16),
        query=struct((count, heads), BF16),
    )
    out_shape = [
        jax.ShapeDtypeStruct(((2 if i == 2 else 1) * x.shape[0], 2) + x.shape[1:], BF16) for i, x in enumerate(shards)
    ]
    out_shape += [jax.ShapeDtypeStruct((count, width), BF16)]
    out_shape += [struct((count, LANES), jnp.int32), struct((8, count), jnp.int32), struct((count, LANES), jnp.int32)]
    out_shape += list(made)
    dma = pltpu.SemaphoreType.DMA
    scratch = [pltpu.VMEM(x.shape, BF16) for x in shards]
    scratch += [dma((n, 5)), dma((n, 4)), dma((5, 2)), dma, dma]
    scratch += [pltpu.VMEM((1,) + blocks[0].shape, BF16), dma((1, 2)), dma((1, 2)), dma((1, 2))]
    scratch += [
        pltpu.VMEM((3, 2) + qkv.shape[1:], BF16),
        pltpu.VMEM((1, 2) + out.shape[1:], BF16),
        pltpu.VMEM((2,) + cross.shape[1:], BF16),
        pltpu.VMEM((1, 2) + ffn_in.shape[1:], BF16),
        pltpu.VMEM((1, 2) + ffn_out.shape[1:], BF16),
    ]
    scratch += [pltpu.VMEM(x.shape, x.dtype) for x in made]
    scratch += [
        pltpu.VMEM((2, count, width), BF16),
        pltpu.VMEM((2, count, width), BF16),
        pltpu.VMEM((count, width), F32),
        pltpu.VMEM((count, count), F32),
        dma((3, 2)),
        dma((5,)),
        dma((len(made),)),
        dma((2, 2)),
    ]
    results = pl.pallas_call(
        functools.partial(head_kernel, tuple(pieces), pairs, scale),
        in_specs=[hbm] * 6 + [vmem, pl.BlockSpec(memory_space=pltpu.SMEM)] + [vmem] * 6,
        out_specs=[hbm] * 5 + [vmem] + [vmem] * 3 + [hbm] * len(made),
        out_shape=out_shape,
        scratch_shapes=scratch,
        compiler_params=pltpu.CompilerParams(
            collective_id=0, has_side_effects=True, vmem_limit_bytes=VMEM_LIMIT
        ),
        name="head",
    )(*shards, *blocks, segment_ids, row_image, *vecs)
    return results[:5], results[5], results[6:9], Head(*results[9:])


CHUNKS = 6


def mid_kernel(pieces, pairs, scale, *refs):
    it = iter(refs)
    act_three, x1, query_in, w_cross_in, w_in_in, w_mlp_in, ffn_shard, cot_block, base = (next(it) for _ in range(9))
    gains, shifts, out_b, ffn_out_b, ffn_in_b, qv_b, picks = (next(it) for _ in range(7))
    d_three, upstream, smalls, tower_out, cross_out = (next(it) for _ in range(5))
    outs = next(it)
    stages = [next(it)]
    weight_sems = [next(it) for _ in range(5)]
    token_stage = next(it)
    token_sems = [next(it) for _ in range(3)]
    images, kv, w_cross, w_in, w_mlp = (next(it) for _ in range(5))
    act_txt, query, mixed, tops, y1, y2, act, pre, hid = (next(it) for _ in range(9))
    grad_hid, raw, grad_pre, g_low, mix_grad, dq, dkv, sum_q = (next(it) for _ in range(8))
    keys, vals, dk, dv = kv.at[0], kv.at[1], dkv.at[0], dkv.at[1]
    cot, part_send, part_recv, halves, half_near, sums, image_grad, own_rows = (next(it) for _ in range(8))
    grads, cross_grad, near, far = (next(it) for _ in range(4))
    red_sems = [next(it) for _ in range(6)]
    load_sem, store_sem, part_sem, twin_sem, side_sem, core_sem, half_sem, sum_sem, back_sem, give_sem, home_sem = it
    tower, dp, z, core, line, other, partner = spots()
    is_enc = tower == 0
    is_dec = tower == 1
    stays = z == 3 * core
    moved = jnp.logical_not(stays)
    side = lax.rem(z, 2)
    across_chip = z + 1 - 2 * side
    count, width = y1.shape
    quarter = count // 2
    chunk = quarter // CHUNKS
    heads = mixed.shape[1]

    home = {DP: 2 * line + z // 2, MP: 2 * lax.rem(z, 2) + core}
    guest = {DP: 2 * line + lax.rem(z, 2), MP: 2 * core + z // 2}
    peers = [(None, {DP: other}), (None, {DP: partner}), (None, {TOWER: 1 - tower})]
    peers += [(None, {MP: lax.rem(z + away, 4)}) for away in range(1, 4)]
    peers += [(moved, home), (moved, guest)]
    barrier_all(peers, [(stays, 6), (moved, 8)])

    def remote(source, target, sends, recvs, where):
        return pltpu.make_async_remote_copy(
            src_ref=source,
            dst_ref=target,
            send_sem=sends,
            recv_sem=recvs,
            device_id=where,
            device_id_type=MESH,
        )

    def span(which_core, i):
        return pl.ds(pl.multiple_of(which_core * quarter + i * chunk, 16), chunk)

    def twin_copy(i):
        rows = span(core, i)
        return remote(
            act_three.at[rows, :], images.at[side, rows, :], twin_sem.at[i, 0], twin_sem.at[i, 1], {TOWER: 1 - tower}
        )

    def side_copy(i, image):
        here = images.at[image, span(core, i), :]
        return remote(here, here, side_sem.at[i, 0], side_sem.at[i, 1], {MP: across_chip})

    def core_copy(i, image, which_core, far_image):
        here = images.at[image, span(which_core, i), :]
        return remote(here, here, core_sem.at[far_image, i, 0], core_sem.at[far_image, i, 1], {DP: partner})

    @pl.when(is_enc)
    def _():
        for i in range(CHUNKS):
            twin_copy(i).start()

    token_begin, token_relay, token_finish = token_steps([cot_block], [cot], token_stage, token_sems)
    pl.when(is_enc)(functools.partial(token_begin, 0))
    begin, begin_local, pass_on, arrived, sent, end_local, _ = weight_steps(
        pieces, [ffn_shard], [w_mlp], stages, weight_sems
    )

    def load(i, source, target):
        return pltpu.make_async_copy(source, target, load_sem.at[i])

    held = pl.ds(0, ffn_shard.shape[1] // 2)
    early = [load(5, w_mlp_in.at[:, :, held, :], w_mlp.at[:, :, held, :])]
    text_loads = [
        load(0, w_cross_in, w_cross),
        load(1, query_in, query),
        load(2, x1, y1),
        load(3, w_in_in, w_in),
        load(4, act_three, act_txt),
    ]

    def part_copy(k, h):
        rows = pl.ds(h * quarter, quarter)
        return remote(
            part_send.at[k % 3, rows, :],
            part_recv.at[k % 3, rows, :],
            part_sem.at[k, h, 0],
            part_sem.at[k, h, 1],
            {DP: partner},
        )

    def home_move():
        return remote(own_rows, tower_out, home_sem.at[0], home_sem.at[1], home)

    def home_stay():
        return pltpu.make_async_copy(own_rows, tower_out, home_sem.at[0])

    def go_home():
        pl.when(moved)(home_move().start)
        pl.when(stays)(home_stay().start)

    def back_copy(i):
        rows = pl.ds(i * chunk, chunk)
        return remote(
            sums.at[1, rows, :], image_grad.at[span(core, i), :], back_sem.at[i, 0], back_sem.at[i, 1], {TOWER: 1 - tower}
        )

    def back_core(i, which_core):
        here = image_grad.at[span(which_core, i), :]
        return remote(here, here, give_sem.at[i, 0], give_sem.at[i, 1], {DP: partner})

    store_grad = pltpu.make_async_copy(y2, upstream, store_sem.at[0])
    store_three = pltpu.make_async_copy(raw, d_three, store_sem.at[1])
    zero = jnp.zeros((8, width), F32)
    blocks, rows_of = grads.shape[0], grads.shape[2]
    red = Reducer(grads, near, far, outs, red_sems, 4, 0, blocks)

    @pl.when(is_enc)
    def _():
        smalls[...] = jnp.zeros_like(smalls)
        mine = pl.ds(pl.multiple_of(core * quarter, TILE), quarter)
        take = load(2, base.at[mine, :], y1.at[pl.ds(0, quarter), :])
        take.start()
        take.wait()

        def lower(rows, kept):
            own_rows[rows, :] = y1[rows, :].astype(BF16)
            return kept

        row_tiles(quarter, lower, 0)
        go_home()
        token_relay(0)
        token_finish(0)

        def lift(rows, kept):
            y2[rows, :] = cot[rows, :].astype(F32)
            return kept

        row_tiles(count, lift, 0)
        store_grad.start()
        for i in range(CHUNKS):
            back_copy(i).wait_recv()
            back_core(i, core).start()
        for i in range(CHUNKS):
            back_core(i, 1 - core).wait_recv()

        def lift_three(rows, kept):
            raw[rows, :] = image_grad[rows, :].astype(F32)
            return kept

        row_tiles(count, lift_three, 0)
        store_three.start()
        for i in range(CHUNKS):
            twin_copy(i).wait_send()
            back_core(i, core).wait_send()

    @pl.when(is_dec)
    def _():
        for one in early + text_loads:
            one.start()
        for one in early:
            one.wait()
        begin_local()
        smalls[...] = jnp.zeros_like(smalls)

        def put(row, value):
            smalls[pl.ds(row, 1), :] = jnp.sum(value, axis=0, keepdims=True)

        for i in range(CHUNKS):
            twin_copy(i).wait_recv()
            side_copy(i, side).start()
            core_copy(i, side, core, 0).start()
        begin()
        for one in text_loads[:2]:
            one.wait()
        mixed[...] = jnp.zeros_like(mixed)
        for i in range(CHUNKS):
            core_copy(i, side, 1 - core, 0).wait_recv()

        @pl.loop(0, 2)
        def _(turn):
            image = side + turn * (1 - 2 * side)

            @pl.when(turn == 1)
            def _():
                for i in range(CHUNKS):
                    side_copy(i, 1 - side).wait_recv()
                    core_copy(i, 1 - side, core, 1).start()
                token_begin(0)
                for i in range(CHUNKS):
                    core_copy(i, 1 - side, 1 - core, 1).wait_recv()

            @pl.loop(0, 2)
            def _(part):
                kv[part, image] = dot_rows(images[image], w_cross[part].reshape(heads, width)).astype(BF16)

            cross_forward(image, query, keys, vals, picks, mixed, tops, pairs, scale)

        for k in range(len(pieces)):
            pass_on(k)
        token_relay(0)

        def half_part(k, made):
            for h in range(2):
                part_send[k % 3, pl.ds(h * quarter, quarter), :] = made(pl.ds(h * quarter, quarter)).astype(BF16)
                part_copy(k, h).start()

        def add_halves(k, run, carry):
            for h in range(2):
                part_copy(k, h).wait()
                carry = row_tiles(quarter, run, carry, h * quarter)
            return carry

        half_part(0, lambda rows: dot_plain(mixed[rows, :], w_cross[3].reshape(heads, width)))
        for one in text_loads[2:]:
            one.wait()
        gain, shift = gains[1], shifts[1]

        def add_cross(rows, kept):
            total = part_send[0, rows, :].astype(F32) + part_recv[0, rows, :].astype(F32)
            value = y1[rows, :] + total
            y2[rows, :] = value
            unit, _ = norm_parts(value)
            act[rows, :] = (unit * gain + shift).astype(BF16)
            return kept

        token_finish(0)
        for k in range(len(pieces)):
            arrived(k)
        end_local(0)

        @pl.loop(0, 2)
        def _(b):
            grad_hid[b] = dot_rows(cot[...], w_mlp[0, b])

        add_halves(0, add_cross, 0)

        @pl.loop(0, 2)
        def _(b):
            cols = pl.ds(pl.multiple_of(b * width, LANES), width)
            pre[...] = dot_plain(act[...], w_in[0, b])
            bias = ffn_in_b[0:1, pl.ds(pl.multiple_of((2 * core + b) * width, LANES), width)]

            def bend(rows, kept):
                lifted, slope = gelu_both(pre[rows, :] + bias)
                hid[rows, cols] = lifted.astype(BF16)
                low = (grad_hid[b, rows, :] * slope).astype(BF16)
                grad_pre[b, rows, :] = low
                return kept + fold_rows(low.astype(F32))

            put(9 + b, row_tiles(count, bend, zero))

        half_part(2, lambda rows: dot_rows(grad_pre[0, rows, :], w_in[0, 0]) + dot_rows(grad_pre[1, rows, :], w_in[0, 1]))

        @pl.loop(0, 2)
        def _(b):
            made = dot_first(grad_pre[b], act[...]).astype(BF16)
            grads[0 : blocks // 2, b] = made.reshape(blocks // 2, rows_of, width)

        red.launch(0)
        red.launch(1)

        def second(rows, kept):
            low_cot = cot[rows, :].astype(F32)
            grad = part_send[2, rows, :].astype(F32) + part_recv[2, rows, :].astype(F32)
            back, dg, db = norm_back_tile(y2[rows, :], gain, grad)
            total = low_cot + back
            raw[rows, :] = total
            g_low[rows, :] = total.astype(BF16)
            return (kept[0] + dg, kept[1] + db, kept[2] + fold_rows(low_cot))

        dg, db, cot_sum = add_halves(2, second, (zero, zero, zero))
        put(3, dg)
        put(6, db)
        put(1, cot_sum)

        mix_grad[...] = dot_rows(g_low[...], w_cross[3].reshape(heads, width)).astype(BF16)
        cross_backward(query, keys, vals, mix_grad, picks, tops, dq, dk, dv, sum_q, pairs, scale)

        def half_copy(image, far_image):
            return remote(
                halves.at[image, pl.ds(pl.multiple_of((1 - core) * quarter, TILE), quarter), :],
                half_near.at[far_image],
                half_sem.at[far_image, 0],
                half_sem.at[far_image, 1],
                {DP: partner},
            )

        @pl.loop(0, 2)
        def _(i):
            image = side + (1 - i) * (1 - 2 * side)
            made = dot_plain(dkv[0, image], w_cross[0].reshape(heads, width))
            made = made + dot_plain(dkv[1, image], w_cross[1].reshape(heads, width))
            halves[image] = made.astype(BF16)
            half_copy(image, 1 - i).start()

        for k in range(2):
            red.add_near(k, False)
            red.launch(k + 2)

        def sum_copy(i):
            rows = pl.ds(i * chunk, chunk)
            return remote(
                sums.at[0, rows, :], sums.at[2, rows, :], sum_sem.at[i, 0], sum_sem.at[i, 1], {MP: across_chip}
            )

        half_copy(1 - side, 1).wait_recv()
        for i in range(CHUNKS):

            def add_far(rows, kept):
                at = pl.ds(pl.multiple_of(i * chunk + rows.start, 16), rows.size)
                own = pl.ds(pl.multiple_of(core * quarter + i * chunk + rows.start, 16), rows.size)
                total = halves[1 - side, own, :].astype(F32) + half_near[1, at, :].astype(F32)
                sums[0, at, :] = total.astype(BF16)
                return kept

            row_tiles(chunk, add_far, 0)
            sum_copy(i).start()
        @pl.loop(0, 2)
        def _(b):
            cols = pl.ds(pl.multiple_of(b * width, LANES), width)
            made = dot_first(hid[:, cols], cot[...]).astype(BF16)
            grads[blocks // 2 : blocks, b] = made.reshape(blocks // 2, rows_of, width)

        red.launch(4)
        red.launch(5)
        half_copy(side, 0).wait_recv()
        for i in range(CHUNKS):
            sum_copy(i).wait_recv()

            def add_own(rows, kept):
                at = pl.ds(pl.multiple_of(i * chunk + rows.start, 16), rows.size)
                own = pl.ds(pl.multiple_of(core * quarter + i * chunk + rows.start, 16), rows.size)
                total = halves[side, own, :].astype(F32) + half_near[0, at, :].astype(F32)
                sums[1, at, :] = (total + sums[2, at, :].astype(F32)).astype(BF16)
                return kept

            row_tiles(chunk, add_own, 0)
            back_copy(i).start()

        half_part(3, lambda rows: dot_plain(dq[rows, :], w_cross[2].reshape(heads, width)))
        red.add_mid(0)
        red.step(2)

        def keep_two(rows, kept):
            y1[rows, :] = raw[rows, :]
            return kept

        row_tiles(count, keep_two, 0)
        pltpu.make_async_copy(y1, upstream, store_sem.at[0]).start()

        def lift_query(rows, kept):
            raw[rows, :] = part_send[0, rows, :].astype(F32) + part_recv[0, rows, :].astype(F32)
            return kept

        add_halves(3, lift_query, 0)
        store_three.start()
        pre[...] = jnp.zeros_like(pre)

        @pl.loop(0, 2)
        def _(b):
            pre[...] += dot_plain(hid[:, pl.ds(pl.multiple_of(b * width, LANES), width)], w_mlp[0, b])

        for h in range(2):
            rows = pl.ds(h * quarter, quarter)
            part_send[1, rows, :] = pre[rows, :].astype(BF16)
            part_copy(1, h).start()
        red.step(3)

        @pl.loop(0, 2)
        def _(which):
            made = dot_first(dkv[which, 0], images[0]) + dot_first(dkv[which, 1], images[1])
            cross_grad[which] = made.astype(BF16).reshape(cross_grad.shape[1:])

        red.step(4)
        cross_grad[2] = dot_first(dq[...], act_txt[...]).astype(BF16).reshape(cross_grad.shape[1:])
        cross_grad[3] = dot_first(mixed[...], g_low[...]).astype(BF16).reshape(cross_grad.shape[1:])
        store_cross = pltpu.make_async_copy(cross_grad, cross_out, store_sem.at[2])
        store_cross.start()
        for h in range(2):
            part_copy(1, h).wait()

        def add_last(rows, kept):
            own = pl.ds(pl.multiple_of(core * quarter + rows.start, 32), rows.size)
            total = part_send[1, own, :].astype(F32) + part_recv[1, own, :].astype(F32)
            own_rows[rows, :] = (y2[own, :] + total + ffn_out_b[...]).astype(BF16)
            return kept

        row_tiles(quarter, add_last, 0)
        go_home()
        red.far_before(5)
        red.drain(5)
        red.close()
        store_cross.wait()
        for i in range(CHUNKS):
            side_copy(i, side).wait_send()
            core_copy(i, side, core, 0).wait_send()
            core_copy(i, 1 - side, core, 1).wait_send()
            sum_copy(i).wait_send()
            back_copy(i).wait_send()
        half_copy(1 - side, 1).wait_send()
        half_copy(side, 0).wait_send()
        for k in range(len(pieces)):
            sent(k)

    pl.when(moved)(home_move().wait)
    pl.when(stays)(home_stay().wait)
    store_grad.wait()
    store_three.wait()


def middle(values, w_cross, w_in, w_mlp, ffn_shard, cot_block, vecs, picks, scale):
    count, width = values.base.shape
    heads = values.mixed.shape[1]
    pairs = heads // LANES
    hidden = values.hid.shape[1]
    quarter = count // 2
    half = width // 2
    chunk = quarter // CHUNKS
    assert chunk * CHUNKS == quarter
    rows_of = heads // 2
    blocks = 2 * (width // rows_of)
    assert hidden == 2 * width
    cross_shape = (4, 2, rows_of, width)
    rows = ffn_shard.shape[1]
    pieces = [(0, 0, 0, 1, at, rows // 4, 1, False) for at in range(rows // 2, rows, rows // 4)]
    n = len(pieces)
    hbm = pl.BlockSpec(memory_space=pltpu.HBM)
    vmem = pl.BlockSpec(memory_space=pltpu.VMEM)
    dma = pltpu.SemaphoreType.DMA
    low, wide = (count, width), (count, heads)
    scratch = [pltpu.VMEM(ffn_shard.shape, BF16), dma((n, 5)), dma((n, 4)), dma((1, 2)), dma, dma]
    scratch += [pltpu.VMEM((1,) + cot_block.shape, BF16), dma((1, 2)), dma((1, 2)), dma((1, 2))]
    scratch += [
        pltpu.VMEM((2,) + low, BF16),
        pltpu.VMEM((2, 2) + wide, BF16),
        pltpu.VMEM((4, 2, heads // 2, width), BF16),
        pltpu.VMEM((1, 2, width, hidden // 2), BF16),
        pltpu.VMEM((1, 2, hidden // 2, width), BF16),
        pltpu.VMEM(low, BF16),
        pltpu.VMEM(wide, BF16),
        pltpu.VMEM(wide, BF16),
        pltpu.VMEM((2, pairs, 8, 2 * count), F32),
        pltpu.VMEM(low, F32),
        pltpu.VMEM(low, F32),
        pltpu.VMEM(low, BF16),
        pltpu.VMEM(low, F32),
        pltpu.VMEM((count, hidden), BF16),
        pltpu.VMEM((2,) + low, F32),
        pltpu.VMEM(low, F32),
        pltpu.VMEM((2, count, hidden // 2), BF16),
        pltpu.VMEM(low, BF16),
        pltpu.VMEM(wide, BF16),
        pltpu.VMEM(wide, BF16),
        pltpu.VMEM((2, 2) + wide, BF16),
        pltpu.VMEM((count, LANES), F32),
        pltpu.VMEM(low, BF16),
        pltpu.VMEM((3,) + low, BF16),
        pltpu.VMEM((3,) + low, BF16),
        pltpu.VMEM((2,) + low, BF16),
        pltpu.VMEM((2, quarter, width), BF16),
        pltpu.VMEM((3, quarter, width), BF16),
        pltpu.VMEM(low, BF16),
        pltpu.VMEM((quarter, width), BF16),
    ]
    scratch += [pltpu.VMEM((blocks, 2, rows_of, width), BF16), pltpu.VMEM(cross_shape, BF16)]
    scratch += [pltpu.VMEM((blocks, 2, rows_of, half), BF16)] * 2
    scratch += [dma((blocks,)), dma((blocks,)), dma((blocks, 2)), dma((blocks, 2)), dma((blocks,)), dma((blocks,))]
    scratch += [
        dma((6,)),
        dma((3,)),
        dma((4, 2, 2)),
        dma((CHUNKS, 2)),
        dma((CHUNKS, 2)),
        dma((2, CHUNKS, 2)),
        dma((2, 2)),
        dma((CHUNKS, 2)),
        dma((CHUNKS, 2)),
        dma((CHUNKS, 2)),
        dma((2,)),
    ]
    out_shape = [
        jax.ShapeDtypeStruct(low, F32),
        jax.ShapeDtypeStruct(low, F32),
        jax.ShapeDtypeStruct((16, width), F32),
        jax.ShapeDtypeStruct((quarter, width), BF16),
        jax.ShapeDtypeStruct(cross_shape, BF16),
        jax.ShapeDtypeStruct((blocks, rows_of, half), BF16),
    ]
    args = [values.act_three, values.x1, values.query, w_cross, w_in, w_mlp]
    return pl.pallas_call(
        functools.partial(mid_kernel, tuple(pieces), pairs, scale),
        in_specs=[hbm] * 9 + [vmem] * 7,
        out_specs=[hbm, hbm, vmem, hbm, hbm, vmem],
        out_shape=out_shape,
        scratch_shapes=scratch,
        compiler_params=pltpu.CompilerParams(
            collective_id=2, has_side_effects=True, vmem_limit_bytes=TAIL_LIMIT
        ),
        name="middle",
    )(*args, ffn_shard, cot_block, values.base, *vecs, picks)


def finish_kernel(*refs):
    it = iter(refs)
    late, early, from_text, total = (next(it) for _ in range(4))
    rows_in = [next(it) for _ in range(2)]
    rows_out = [next(it) for _ in range(2)]
    o_qkv, o_out, o_in, o_mlp, o_cross, o_qv, o_outb, o_inb, o_mlpb, o_gain, o_shift = (next(it) for _ in range(11))
    held = [next(it) for _ in range(2)]
    b_in, b_mlp, b_out, b_qkv, b_cross, sem = it
    tower, dp, z, core, line, other, partner = spots()

    def bring(i, image_src, text_src, target):
        @pl.when(tower == 0)
        def _():
            pltpu.make_async_copy(image_src, target, sem.at[i]).start()

        @pl.when(tower == 1)
        def _():
            pltpu.make_async_copy(text_src, target, sem.at[i]).start()

    n = b_in.shape[0]
    bring(0, late.at[pl.ds(n, n)], early.at[pl.ds(0, n)], b_in)
    bring(1, late.at[pl.ds(0, n)], early.at[pl.ds(n, n)], b_mlp)
    bring(2, late.at[2 * n], late.at[2 * n], b_out)
    bring(3, late.at[pl.ds(2 * n + 1, 3)], late.at[pl.ds(2 * n + 1, 3)], b_qkv)
    bring(4, from_text, late.at[pl.ds(n + 2, 2)], b_cross)
    for i in range(2):
        pltpu.make_async_copy(rows_in[i], held[i], sem.at[5 + i]).start()

    width = total.shape[2]
    heads = width // 2
    first = total[0]
    o_outb[...] = first[0:1, :]
    o_mlpb[...] = first[1:2, :]
    for i in range(3):
        o_gain[i] = first[2 + i : 3 + i, :]
        o_shift[i] = first[5 + i : 6 + i, :]
    for side in range(2):
        lanes = slice(side * heads, (side + 1) * heads)
        o_qv[0, 0:1, lanes] = total[side, 8:9, :heads]
        o_qv[0, 1:2, lanes] = total[side, 8:9, heads:]
        for b in range(2):
            at = (2 * side + b) * width
            o_inb[0:1, at : at + width] = total[side, 9 + b : 10 + b, :]

    def mine(block):
        cut = block.shape[1] // 2
        wide = block.astype(F32)
        return jnp.where(core == 0, wide[:, :cut], wide[:, cut:])

    for i in range(2):
        pltpu.make_async_copy(rows_in[i], held[i], sem.at[5 + i]).wait()
        pltpu.make_async_copy(held[i], rows_out[i].at[0], sem.at[7 + i]).start()
    half = b_in.shape[2]
    cols = b_in.shape[1]
    pltpu.make_async_copy(late.at[pl.ds(0, n)], b_in, sem.at[0]).wait()
    for i in range(n // 2):
        pair = b_in[2 * i : 2 * i + 2].reshape(2 * cols, half)
        o_in[0, :, 2 * i * cols : 2 * (i + 1) * cols] = mine(pair).T
    pltpu.make_async_copy(late.at[pl.ds(0, n)], b_mlp, sem.at[1]).wait()
    for i in range(n // 2):
        pair = b_mlp[2 * i : 2 * i + 2].reshape(2 * cols, half)
        o_mlp[0, :, 2 * i * cols : 2 * (i + 1) * cols] = mine(pair).T
    pltpu.make_async_copy(late.at[0], b_out, sem.at[2]).wait()
    o_out[0] = mine(b_out[...])
    pltpu.make_async_copy(late.at[pl.ds(0, 3)], b_qkv, sem.at[3]).wait()
    for a in range(3):
        o_qkv[0, a] = mine(b_qkv[a]).T
    pltpu.make_async_copy(late.at[pl.ds(0, 2)], b_cross, sem.at[4]).wait()
    for a in range(2):
        o_cross[0, a] = mine(b_cross[a]).T
    for i in range(2):
        pltpu.make_async_copy(held[i], rows_out[i].at[0], sem.at[7 + i]).wait()


def finish(late, early, from_text, total, token_rows):
    hbm = pl.BlockSpec(memory_space=pltpu.HBM)
    vmem = pl.BlockSpec(memory_space=pltpu.VMEM)
    struct = jax.ShapeDtypeStruct
    width = total.shape[2]
    blocks, cols, half = early.shape
    n = blocks // 2
    ffn, cut = n * cols, half // 2
    out_shape = [struct((1,) + x.shape, BF16) for x in token_rows]
    out_shape += [
        struct((1, 3, cut, cols), F32),
        struct((1, cols, cut), F32),
        struct((1, cut, ffn), F32),
        struct((1, cut, ffn), F32),
        struct((1, 2, cut, cols), F32),
        struct((1, 2, width), F32),
        struct((1, width), F32),
        struct((1, 4 * width), F32),
        struct((1, width), F32),
        struct((3, 1, width), F32),
        struct((3, 1, width), F32),
    ]
    scratch = [pltpu.VMEM(x.shape, BF16) for x in token_rows]
    scratch += [pltpu.VMEM(x + (cols, half), BF16) for x in ((n,), (n,), (), (3,), (2,))]
    scratch += [pltpu.SemaphoreType.DMA((9,))]
    results = pl.pallas_call(
        finish_kernel,
        in_specs=[hbm] * 3 + [vmem] + [hbm] * 2,
        out_specs=[hbm] * 2 + [vmem] * 11,
        out_shape=out_shape,
        scratch_shapes=scratch,
        compiler_params=pltpu.CompilerParams(vmem_limit_bytes=VMEM_LIMIT),
        name="finish",
    )(late, early, from_text, total, *token_rows)
    turned = {5: (1, 2), 11: (0, 1), 12: (0, 1)}
    return tuple(jnp.swapaxes(x, *turned[i]) if i in turned else x for i, x in enumerate(results))


def split_heads(flat):
    return jnp.swapaxes(flat.reshape(flat.shape[0], -1, HDIM), 0, 1)


def join_heads(split):
    return jnp.swapaxes(split, 0, 1).reshape(split.shape[1], -1)


def batch_dot(left, right, left_dim, right_dim):
    return lax.dot_general(left, right, (((left_dim,), (right_dim,)), ((0,), (0,))), preferred_element_type=F32)


def attend_plain(queries, keys, vals, allowed, scale):
    queries, keys, vals = (split_heads(x) for x in (queries, keys, vals))
    scores = jnp.where(allowed, batch_dot(queries, keys, 2, 2) * scale, NEG)
    top = jnp.max(scores, axis=-1, keepdims=True)
    tops = top + jnp.log(jnp.sum(jnp.exp(scores - top), axis=-1, keepdims=True))
    weights = jnp.exp(scores - tops).astype(BF16)
    return (join_heads(batch_dot(weights, vals, 2, 1)).astype(BF16), tops)


def attend_back_plain(queries, keys, vals, grads, tops, allowed, scale):
    queries, keys, vals, grads = (split_heads(x) for x in (queries, keys, vals, grads))
    scores = jnp.where(allowed, batch_dot(queries, keys, 2, 2) * scale, NEG)
    weights = jnp.exp(scores - tops)
    grad_w = batch_dot(grads, vals, 2, 2)
    grad_s = (weights * (grad_w - jnp.sum(weights * grad_w, axis=-1, keepdims=True))).astype(BF16)
    return (
        join_heads(batch_dot(grad_s, keys, 2, 1) * scale).astype(BF16),
        join_heads(batch_dot(grad_s, queries, 1, 1) * scale).astype(BF16),
        join_heads(batch_dot(weights.astype(BF16), grads, 1, 1)).astype(BF16),
    )


def gather_plain(shards):
    core = lax.rem(lax.axis_index(DP), 2)
    outs = []
    for i, s in enumerate(shards):
        if i == 2:
            s = jnp.concatenate([lax.ppermute(s, TOWER, [(0, 1)]), s], axis=0)
        full = lax.all_gather(s, MP, axis=1, tiled=False)
        outs.append(lax.dynamic_slice_in_dim(full, 2 * core, 2, 1))
    return outs


def reduce_plain(grads, smalls):
    dp = lax.axis_index(DP)
    core = lax.rem(dp, 2)
    outs = []
    for g in grads:
        n, _, rows, wide = g.shape
        full = jnp.zeros((n, 4, rows, wide), BF16)
        full = lax.dynamic_update_slice(full, g, (0, 2 * core, 0, 0))
        part = lax.psum_scatter(full, MP, scatter_dimension=1, tiled=False)
        part = lax.psum_scatter(part, DP, scatter_dimension=2, tiled=True)
        outs.append(part)
    if smalls is None:
        return outs
    both = jnp.zeros((2,) + smalls.shape, F32)
    both = lax.dynamic_update_slice(both, smalls[None], (core, 0, 0))
    return outs + [lax.psum(both, (DP, MP))]


def body(
    tower_in,
    out_cot,
    segment_ids,
    row_image,
    attn_qkv,
    attn_out,
    mlp_in,
    mlp_out,
    cross_proj,
    qv_bias,
    out_bias,
    mlp_bias_in,
    mlp_bias_out,
    norm_gain,
    norm_bias,
):
    lines = lax.axis_size(DP) // 2
    depth = lax.axis_size(MP)
    devices = lax.axis_size(DP)
    is_enc = lax.axis_index(TOWER) == 0
    dp = lax.axis_index(DP)
    z = lax.axis_index(MP)
    core = lax.rem(dp, 2)
    side = lax.rem(z, 2)
    group = z // 2
    direct = lines == 2
    assert depth == 4
    quarter = tower_in.shape[1]
    tokens = 2 * quarter
    assert tokens == PATCH
    width = tower_in.shape[2]
    head_cols = 2 * attn_qkv.shape[3]
    hidden = 2 * mlp_in.shape[2]
    scale_qk = HDIM ** (-0.5)

    out_moves, back_moves = [], []
    for d in range(devices):
        for place in range(depth):
            here = d * depth + place
            there = (d - d % 2 + place % 2) * depth + 2 * (d % 2) + place // 2
            out_moves.append((here, there))
            back_moves.append((there, here))

    def swap_cores(x):
        return lax.ppermute(x, DP, [(i, i ^ 1) for i in range(devices)])

    def both_cores(own):
        other = swap_cores(own)
        return jnp.where(core == 0, jnp.concatenate([own, other], -2), jnp.concatenate([other, own], -2))

    def own_rows(full):
        return lax.dynamic_slice_in_dim(full, core * quarter, quarter, full.ndim - 2)

    def lowered(part):
        return lax.reduce_precision(part, 8, 7).astype(BF16)

    def add_lowered(low):
        return low.astype(F32) + swap_cores(low).astype(F32)

    def add_cores(part):
        return add_lowered(lowered(part))

    def only_image(run, *operands):
        def idle(*inputs):
            return jax.tree.map(lambda x: jnp.zeros(x.shape, x.dtype), jax.eval_shape(run, *inputs))

        return lax.cond(is_enc, run, idle, *operands)

    shards = [
        jnp.swapaxes(attn_qkv[0], 1, 2),
        attn_out,
        jnp.swapaxes(cross_proj[0], 1, 2),
        mlp_in,
        mlp_out,
    ]
    rows = segment_ids.shape[0] // 2

    bias_qv = lax.dynamic_slice_in_dim(qv_bias[0], core * head_cols, head_cols, 1)
    bias_packed = jnp.concatenate([bias_qv[0], jnp.zeros_like(bias_qv[0]), bias_qv[1]])
    bias_in = lax.dynamic_slice_in_dim(mlp_bias_in[0], core * hidden, hidden, 0)
    gains = norm_gain[0]
    shifts = norm_bias[0]

    def feed_forward(values):
        act = norm_rows(values, gains[1], shifts[1]).astype(BF16)
        pre = jnp.concatenate([dot_plain(act, w_in[0]), dot_plain(act, w_in[1])], axis=1) + bias_in
        hid = gelu_tanh(pre).astype(BF16)
        return (act, pre, hid, lowered(dot_plain(hid, w_mlp)))

    if direct:
        tall_gains, tall_shifts = (jnp.swapaxes(x, 0, 1) for x in (norm_gain, norm_bias))
        vecs = (tall_gains, tall_shifts, out_bias, mlp_bias_out, mlp_bias_in, qv_bias[0])
        gathered, stream_low, notes, first = head(
            shards, [tower_in[0]], segment_ids, row_image, vecs, scale_qk
        )
        seg_col, seg_row, picks = notes
    else:
        gathered = gather_plain(shards)
        stream_low = both_cores(lax.ppermute(tower_in[0], (DP, MP), out_moves))
        cot_low = both_cores(lax.ppermute(out_cot[0], (DP, MP), out_moves))
        segs = jnp.where(core == group, segment_ids, swap_cores(segment_ids))
        segs = lax.dynamic_slice_in_dim(segs, rows * side, rows, 0)
        marks = (segs + LTXT * jnp.arange(rows, dtype=jnp.int32)[:, None]).reshape(tokens)
        images_of = jnp.where(core == group, row_image, swap_cores(row_image))
        images_of = jnp.repeat(lax.dynamic_slice_in_dim(images_of, rows * side, rows, 0), LTXT)
        places = jnp.arange(tokens)
        allowed = (places[None, :] <= places[:, None]) & (marks[None, :] == marks[:, None])
        allowed = jnp.logical_or(allowed, is_enc)
        sees = images_of[:, None] == jnp.arange(2 * tokens)[None, :] // tokens
    w_qkv = gathered[0].reshape(3 * head_cols, width)
    w_out = gathered[1].reshape(head_cols, width)
    w_cross = gathered[2].reshape(4, head_cols, width)
    w_in = gathered[3][0]
    w_mlp = gathered[4].reshape(hidden, width)
    stream = stream_low.astype(F32)

    if not direct:
        act_one = norm_rows(stream, gains[0], shifts[0]).astype(BF16)
        packed = (dot_rows(act_one, w_qkv) + bias_packed).astype(BF16)
        parts = [packed[:, i * head_cols : (i + 1) * head_cols] for i in range(3)]
        mixed, tops = attend_plain(*parts, allowed, scale_qk)
        stream_one = stream + add_cores(dot_plain(mixed, w_out)) + out_bias[0]
        act_enc, pre_enc, hid_enc, part_enc = feed_forward(stream_one)
        out_enc = stream_one + add_lowered(part_enc) + mlp_bias_out[0]
        base_three = jnp.where(is_enc, out_enc, stream_one)
        act_three = norm_rows(base_three, gains[2], shifts[2]).astype(BF16)
        cross_q = dot_rows(act_three, w_cross[2]).astype(BF16)

    if direct:
        back_in_three, upstream, smalls, tower_out, g_cross, early = middle(
            first, gathered[2], gathered[3], gathered[4], mlp_out, out_cot[0], vecs, picks, scale_qk
        )
        values = Tail(
            d_three=back_in_three,
            base=first.base,
            upstream=upstream,
            gains=tall_gains,
            smalls=smalls,
            w_mlp=w_mlp,
            pre=first.pre,
            hid=first.hid,
            act=first.act,
            w_in=w_in,
            x1=first.x1,
            w_out=w_out,
            mixed=first.mixed,
            packed=first.packed,
            tops=first.tops,
            seg_col=seg_col,
            seg_row=seg_row,
            a_one=first.a_one,
            w_qkv=w_qkv,
            x0=stream_low,
        )
        late, total, grad_in, from_text = tail(values, g_cross, scale_qk)
        return finish(late, early, from_text, total, [tower_out, grad_in])
    else:
        near_half = lax.ppermute(own_rows(act_three), TOWER, [(0, 1)])
        far_half = lax.ppermute(near_half, MP, [(i, i ^ 1) for i in range(depth)])
        halves = jnp.where(side == 0, jnp.stack([near_half, far_half]), jnp.stack([far_half, near_half]))
        images = both_cores(halves)

        flat_images = images.reshape(2 * tokens, width)
        cross_k = dot_rows(flat_images, w_cross[0]).astype(BF16)
        cross_v = dot_rows(flat_images, w_cross[1]).astype(BF16)
        cross_mix, cross_tops = attend_plain(cross_q, cross_k, cross_v, sees, scale_qk)
        stream_two = stream_one + add_cores(dot_plain(cross_mix, w_cross[3]))

        act_dec, pre_dec, hid_dec, part_dec = feed_forward(stream_two)
        out_dec = stream_two + add_lowered(part_dec) + mlp_bias_out[0]
        tower_rows = own_rows(jnp.where(is_enc, base_three, out_dec).astype(BF16))

        def feed_back(grad_low, pre):
            grad_hid = dot_rows(grad_low, w_mlp)
            _, pullback = jax.vjp(gelu_tanh, pre)
            grad_pre = pullback(grad_hid)[0].astype(BF16)
            cols = hidden // 2
            part = dot_rows(grad_pre[:, :cols], w_in[0]) + dot_rows(grad_pre[:, cols:], w_in[1])
            return (grad_pre, lowered(part))

        def feed_grads(grad_low, act, grad_pre, hid):
            g_in = dot_first(grad_pre, act).astype(BF16)
            g_mlp = dot_first(hid, grad_low).astype(BF16)
            return (
                g_in.reshape(1, 2, hidden // 2, width),
                g_mlp.reshape(1, 2, hidden // 2, width),
            )

        cot = cot_low.astype(F32)
        grad_pre_dec, back_in = feed_back(cot_low, pre_dec)
        back_a, gain_a, shift_a = norm_back(stream_two, gains[1], add_lowered(back_in))
        grad_two = cot + back_a
        grad_two_low = grad_two.astype(BF16)

        grad_mix = dot_rows(grad_two_low, w_cross[3]).astype(BF16)
        grad_q, flat_k, flat_v = attend_back_plain(
            cross_q, cross_k, cross_v, grad_mix, cross_tops, sees, scale_qk
        )
        part_images = dot_plain(flat_k, w_cross[0]) + dot_plain(flat_v, w_cross[1])
        part_low = part_images.astype(BF16).reshape(2, 2, quarter, width)
        give = lax.dynamic_index_in_dim(part_low, 1 - core, 1, keepdims=False)
        keep = lax.dynamic_index_in_dim(part_low, core, 1, keepdims=False)
        pair_sum = (keep.astype(F32) + swap_cores(give).astype(F32)).astype(BF16)
        give = lax.dynamic_index_in_dim(pair_sum, 1 - side, 0, keepdims=False)
        keep = lax.dynamic_index_in_dim(pair_sum, side, 0, keepdims=False)
        got = lax.ppermute(give, MP, [(i, i ^ 1) for i in range(depth)])
        image_sum = (keep.astype(F32) + got.astype(F32)).astype(BF16)
        image_half = lax.ppermute(image_sum, TOWER, [(1, 0)])
        later = lax.optimization_barrier(
            (cot_low, act_dec, grad_pre_dec, hid_dec, flat_k, flat_v, grad_q, cross_mix, image_sum)
        )
        g_in_dec, g_mlp_dec = feed_grads(later[0], later[1], later[2], later[3])
        g_cross = jnp.concatenate(
            [
                dot_first(later[4], flat_images).astype(BF16),
                dot_first(later[5], flat_images).astype(BF16),
                dot_first(later[6], act_three).astype(BF16),
                dot_first(later[7], grad_two_low).astype(BF16),
            ],
            axis=0,
        ).reshape(4, 2, head_cols // 2, width)
        image_back = both_cores(image_half).astype(F32)
        query_back = add_cores(dot_plain(grad_q, w_cross[2]))
        back_in_three = jnp.where(is_enc, image_back, query_back)
        text_smalls = (
            jnp.zeros((16, width), F32)
            .at[1]
            .set(jnp.sum(cot_low, axis=0, dtype=F32))
            .at[3]
            .set(gain_a)
            .at[6]
            .set(shift_a)
            .at[9:11]
            .set(jnp.sum(grad_pre_dec, axis=0, dtype=F32).reshape(2, width))
        )
        smalls = jnp.where(is_enc, 0.0, text_smalls)
        tower_out = lax.ppermute(tower_rows, (DP, MP), back_moves)
        back_three, gain_three, shift_three = norm_back(
            base_three, gains[2], back_in_three
        )
        grad_enc = cot + back_three
        grad_enc_low = grad_enc.astype(BF16)

        grad_pre_enc, back_in = feed_back(grad_enc_low, pre_enc)
        g_in, g_mlp = feed_grads(grad_enc_low, act_enc, grad_pre_enc, hid_enc)
        back_b, gain_b, shift_b = norm_back(stream_one, gains[1], add_lowered(back_in))
        grad_one = jnp.where(is_enc, grad_enc + back_b, grad_two + back_three)
        grad_one_low = grad_one.astype(BF16)

        g_out = dot_first(mixed, grad_one_low).astype(BF16).reshape(1, 2, head_cols // 2, width)
        grad_mixed = dot_rows(grad_one_low, w_out).astype(BF16)
        grad_packed = jnp.concatenate(
            attend_back_plain(*parts, grad_mixed, tops, allowed, scale_qk), axis=1
        )
        g_qkv = dot_first(grad_packed, act_one).astype(BF16).reshape(3, 2, head_cols // 2, width)
        back_in = add_cores(dot_plain(grad_packed, w_qkv))
        back_one, gain_one, shift_one = norm_back(stream, gains[0], back_in)
        grad_in = own_rows((grad_one + back_one).astype(BF16))
        grad_in = lax.ppermute(grad_in, (DP, MP), back_moves)

        grad_pre_sum = jnp.sum(grad_pre_enc, axis=0, dtype=F32).reshape(2, width)
        packed_sum = jnp.sum(grad_packed, axis=0, dtype=F32)
        smalls = jnp.concatenate(
            [
                jnp.sum(grad_one_low, axis=0, dtype=F32)[None],
                jnp.where(is_enc, jnp.sum(grad_enc_low, axis=0, dtype=F32), smalls[1])[None],
                gain_one[None],
                jnp.where(is_enc, gain_b, smalls[3])[None],
                gain_three[None],
                shift_one[None],
                jnp.where(is_enc, shift_b, smalls[6])[None],
                shift_three[None],
                jnp.concatenate([packed_sum[:head_cols], packed_sum[2 * head_cols :]])[None],
                jnp.where(is_enc, grad_pre_sum, smalls[9:11]),
                smalls[11:],
            ]
        )
        g_in = jnp.where(is_enc, g_in, g_in_dec)
        g_mlp = jnp.where(is_enc, g_mlp, g_mlp_dec)
        s_in, s_mlp, s_out, s_qkv, s_cross, total = reduce_plain([g_in, g_mlp, g_out, g_qkv, g_cross], smalls)
        s_cross = jnp.where(is_enc, lax.ppermute(s_cross[:2], TOWER, [(1, 0)]), s_cross[2:])

    def turned(x):
        return jnp.swapaxes(x, 1, 2).astype(F32)

    cross_pair = jnp.stack(
        [
            s_cross[0].T,
            s_cross[1].T,
        ]
    ).astype(F32)
    first = total[0]
    qv_total = jnp.stack(
        [
            total[:, 8, :head_cols].reshape(-1),
            total[:, 8, head_cols:].reshape(-1),
        ]
    )
    in_total = total[:, 9:11].reshape(-1)
    return (
        tower_out[None],
        grad_in[None],
        turned(s_qkv)[None],
        s_out.astype(F32),
        turned(s_in),
        s_mlp.astype(F32),
        cross_pair[None],
        qv_total[None],
        first[0:1],
        in_total[None],
        first[1:2],
        first[2:5][None],
        first[5:8][None],
    )


def solution(mesh):
    return jax.shard_map(
        body,
        mesh=mesh,
        in_specs=(
            P(TOWER, (DP, MP), None),
            P(TOWER, (DP, MP), None),
            P(DP, None),
            P(DP),
            P(TOWER, None, None, MP),
            P(TOWER, MP, None),
            P(TOWER, None, MP),
            P(TOWER, MP, None),
            P(TOWER, None, None, MP),
            P(TOWER, None, None),
            P(TOWER, None),
            P(TOWER, None),
            P(TOWER, None),
            P(TOWER, None, None),
            P(TOWER, None, None),
        ),
        out_specs=(
            P(TOWER, (DP, MP), None),
            P(TOWER, (DP, MP), None),
            P(TOWER, None, DP, MP),
            P(TOWER, MP, DP),
            P(TOWER, DP, MP),
            P(TOWER, MP, DP),
            P(TOWER, None, DP, MP),
            P(TOWER, None, None),
            P(TOWER, None),
            P(TOWER, None),
            P(TOWER, None),
            P(TOWER, None, None),
            P(TOWER, None, None),
        ),
        check_vma=False,
    )
```

profile of v0, /device:TPU:11, one launch (start us, length us, event | category | flops | bytes accessed | tf_op | source)
XLA Modules:
  0.0 336.0 jit_solution(17174713148631583945)
XLA Ops:
  0.6 96.0 %head.1 = (bf16[3,2,192,768]{3,2,1,0:T(8,128)(2,1)}, bf16[1,2,192,768]{3,2,1,0:T(8,128)(2,1)}, bf16[4,2,192,768]{3,2,1,0:T(8,128)(2,1)}, bf16[1,2,768,768]{3,2,1...) custom-call(bf16[3,192,768]{2,1,0:T(8,128)(2,1)} %bitcast.21, ...), custom_call_target="tpu_custom_call" | custom-call | tf_op jit(solution)/shard_map/head/pallas_call | solution.py:1392
  96.7 148.7 %middle.1 = (f32[576,768]{1,0:T(8,128)}, f32[576,768]{1,0:T(8,128)}, f32[16,768]{1,0:T(8,128)}, bf16[288,768]{1,0:T(8,128)(2,1)}, bf16[4,2,192,768]{3,2,1,0:T(8,128)(2,1)}, /*index=5*/bf16[8,192,384]{2,1,0:T(8,128)(2,1)}) custom-call(bf16[576,768]{1,0:T(8,128)(2,1)} %get-tuple-element.56.refs_0_, f32[576,768]{1,0:T(8,128)} %get-tuple-element.57.refs_1_.refs_10_, ...), custom_call_target="tpu_custom_call" | custom-call | tf_op jit(solution)/shard_map/middle/pallas_call | solution.py:1906
  245.3 84.9 %tail.1 = (bf16[12,192,384]{2,1,0:T(8,128)(2,1)}, f32[2,16,768]{2,1,0:T(8,128)}, bf16[288,768]{1,0:T(8,128)(2,1)}, bf16[2,192,384]{2,1,0:T(8,128)(2,1)}) custom-call(f32[576,768]{1,0:T(8,128)} %get-tuple-element.64.refs_0_, f32[576,768]{1,0:T(8,128)} %get-tuple-element.62.refs_8_.refs_1_, f32[576,768]{1,0:T(8,128)} %get-tuple-element.65.refs_2_, ...), custom_call_target="tpu_custom_call" | custom-call | tf_op jit(solution)/shard_map/tail/pallas_call | solution.py:1044
  330.3 5.6 %finish.1 = (bf16[1,288,768]{2,1,0:T(8,128)(2,1)}, bf16[1,288,768]{2,1,0:T(8,128)(2,1)}, f32[1,3,192,192]{3,2,1,0:T(8,128)}, f32[1,192,192]{2,1,0:T(8,128)}, f32...) custom-call(bf16[12,192,384]{2,1,0:T(8,128)(2,1)} %get-tuple-element, ...), custom_call_target="tpu_custom_call" | custom-call | tf_op jit(solution)/shard_map/finish/pallas_call | solution.py:2018
where the time goes:
time: 340 us; the launch traced here: 336 us
  Pallas kernels  335 us (99%)
    pallas_call x1, Pallas kernels, middle(): pl.pallas_call(functools.partial(mid_kernel, tuple(pieces), pairs, scale)...  149 us
    pallas_call x1, Pallas kernels, head(): pl.pallas_call(functools.partial(head_kernel, tuple(pieces), pairs, scale...  96 us
    pallas_call x1, Pallas kernels, tail(): pl.pallas_call(functools.partial(tail_kernel, pairs, scale), in_specs=[hb...  84.9 us

commit v1 on v0

--- a/solution.py
+++ b/solution.py
@@ -517,7 +517,7 @@
 
 
 class Reducer:
-    def __init__(self, grads, near, far, outs, sems, window, first, last):
+    def __init__(self, grads, near, far, outs, sems, window, first, last, near_last):
         self.grads, self.near, self.far, self.outs = grads, near, far, outs
         self.y_send, self.y_recv, self.z_send, self.z_recv, self.c_send, self.c_recv = sems
         self.tower, self.dp, self.z, self.core, self.line, self.other, self.partner = spots()
@@ -526,7 +526,7 @@
         self.slot = lax.rem(self.z, 2)
         self.half = grads.shape[3] // 2
         self.rows = grads.shape[2]
-        self.window, self.first, self.last = window, first, last
+        self.window, self.first, self.last, self.near_last = window, first, last, near_last
 
     def lanes(self, line):
         return pl.ds(pl.multiple_of(line * self.half, LANES), self.half)
@@ -582,7 +582,7 @@
         self.to_line(k).wait_send()
         self.to_line(k).wait_recv()
         if more:
-            pl.when(k + self.window < self.last)(lambda: self.launch(k + self.window))
+            pl.when(k + self.window < self.near_last)(lambda: self.launch(k + self.window))
 
         def run(rows):
             for b in range(2):
@@ -590,6 +590,10 @@
                 self.near[k, b, rows, :] = total.astype(BF16)
 
         self.tiles(run)
+        if more:
+            pl.when(k < self.last)(lambda: self.hop(k))
+
+    def hop(self, k):
         pl.when(self.place == 3)(self.inward(k).start)
         pl.when(self.holder)(self.beside(k).start)
 
@@ -622,18 +626,19 @@
             self.tiles(run)
             self.to_core(k).start()
 
-    def step(self, k):
+    def step(self, k, mid=1):
         self.add_near(k)
-        pl.when(k - LAG >= self.first)(lambda: self.add_mid(k - LAG))
+        if mid:
+            pl.when(k - LAG >= self.first)(lambda: self.add_mid(k - LAG))
 
     def drain(self, begin):
-        @pl.loop(begin, self.last + 2 * LAG)
+        @pl.loop(begin, max(self.near_last, self.last + 2 * LAG))
         def _(i):
-            pl.when(i < self.last)(lambda: self.add_near(i))
+            pl.when(i < self.near_last)(lambda: self.add_near(i))
             j = i - LAG
             pl.when(jnp.logical_and(j >= self.first, j < self.last))(lambda: self.add_mid(j))
             n = j - LAG
-            pl.when(jnp.logical_and(n >= begin - 2 * LAG, n >= self.first))(lambda: self.add_far(n))
+            pl.when(jnp.logical_and(n < self.last, n >= self.first))(lambda: self.add_far(n))
 
     def far_before(self, begin):
         @pl.loop(self.first, jnp.maximum(self.first, begin - 2 * LAG))
@@ -689,9 +694,9 @@
 def tail_kernel(pairs, scale, *refs):
     it = iter(refs)
     hbm = Tail(*[next(it) for _ in Tail._fields])
-    cross_in = next(it)
+    cross_in, tower_rows = next(it), next(it)
     outs = next(it)
-    small_out, grad_out, from_text = next(it), next(it), next(it)
+    small_out, grad_out, from_text, tower_out = next(it), next(it), next(it), next(it)
     vm = Tail(*[next(it) for _ in Tail._fields])
     grads, near, far = next(it), next(it), next(it)
     g_f32, g_low, grad_hid, grad_pre, d_packed, mix_grad = (next(it) for _ in range(6))
@@ -707,6 +712,7 @@
     heads = mix_grad.shape[1]
     rows_of = grads.shape[2]
     ffn_blocks = width // rows_of
+    text_first = 2 * ffn_blocks - 2
 
     home = {DP: 2 * line + z // 2, MP: 2 * lax.rem(z, 2) + core}
     guest = {DP: 2 * line + lax.rem(z, 2), MP: 2 * core + z // 2}
@@ -733,7 +739,7 @@
         else:
             run()
 
-    pl.when(is_dec)(lambda: pltpu.make_async_copy(cross_in, grads.at[pl.ds(ffn_blocks, ffn_blocks)], load_sem.at[len(hbm)]).start())
+    pl.when(is_dec)(lambda: pltpu.make_async_copy(cross_in, near.at[pl.ds(text_first, 2)], load_sem.at[len(hbm)]).start())
     for i in range(len(hbm)):
         on_side(i, load(i).start)
 
@@ -742,13 +748,13 @@
             if any(ref is one for one in wanted):
                 on_side(i, load(i).wait)
 
-    first_block = ffn_blocks * tower
+    first_block = text_first * tower
     blocks = grads.shape[0]
-    red = Reducer(grads, near, far, outs, red_sems, 2, first_block, blocks)
+    red = Reducer(grads, near, far, outs, red_sems, 2 + tower, first_block, blocks, blocks)
 
     def twin_copy():
         return pltpu.make_async_remote_copy(
-            src_ref=outs.at[pl.ds(ffn_blocks, 2)],
+            src_ref=outs.at[pl.ds(text_first, 2)],
             dst_ref=from_text,
             send_sem=twin_sem.at[0],
             recv_sem=twin_sem.at[1],
@@ -756,12 +762,13 @@
             device_id_type=MESH,
         )
 
-    cross_load = pltpu.make_async_copy(cross_in, grads.at[pl.ds(ffn_blocks, ffn_blocks)], load_sem.at[len(hbm)])
+    cross_load = pltpu.make_async_copy(cross_in, near.at[pl.ds(text_first, 2)], load_sem.at[len(hbm)])
 
     @pl.when(is_dec)
     def _():
         cross_load.wait()
-        red.launch(ffn_blocks)
+        red.hop(text_first)
+        red.hop(text_first + 1)
 
     def home_move(source, target, k):
         return pltpu.make_async_remote_copy(
@@ -773,6 +780,17 @@
             device_id_type=MESH,
         )
 
+    @pl.when(moved)
+    def _():
+        home_move(tower_rows, tower_out, 0).start()
+
+    @pl.when(stays)
+    def _():
+        pltpu.make_async_copy(tower_rows, own_grad, move_sem.at[0, 0]).start()
+        pltpu.make_async_copy(tower_rows, own_grad, move_sem.at[0, 0]).wait()
+        pltpu.make_async_copy(own_grad, tower_out, move_sem.at[0, 1]).start()
+        pltpu.make_async_copy(own_grad, tower_out, move_sem.at[0, 1]).wait()
+
     def part_copy(k):
         return pltpu.make_async_remote_copy(
             src_ref=part_send.at[k],
@@ -869,30 +887,61 @@
     @pl.when(is_dec)
     def _():
         put(0, bias)
-        red.launch(ffn_blocks + 1)
 
     need(vm.w_out, vm.mixed, vm.packed, vm.tops, vm.seg_col, vm.seg_row)
     mix_grad[...] = dot_rows(g_low[...], vm.w_out[...]).astype(BF16)
     grads[2 * ffn_blocks] = dot_first(vm.mixed[...], g_low[...]).astype(BF16).reshape(grads.shape[1:])
-    now = 2 + (ffn_blocks - 2) * tower
 
     fill_mask(mask, vm.seg_col, vm.seg_row, is_dec)
-    red.step(now)
-    self_backward(vm.packed, mix_grad, vm.tops, mask, d_packed, pairs, scale, lambda: red.step(now + 1))
-    red.step(now + 2)
+
+    @pl.when(is_enc)
+    def _():
+        red.step(2)
+
+    @pl.when(is_dec)
+    def _():
+        red.launch(2 * ffn_blocks)
+
+    def between():
+        @pl.when(is_enc)
+        def _():
+            red.step(3)
+
+    self_backward(vm.packed, mix_grad, vm.tops, mask, d_packed, pairs, scale, between)
+
+
+    @pl.when(is_enc)
+    def _():
+        red.step(4)
+
+    @pl.when(is_dec)
+    def _():
+        red.add_mid(text_first)
+
+    now = 5 + (2 * ffn_blocks - 5) * tower
 
 
     need(vm.a_one, vm.w_qkv, vm.x0)
-    grad_hid[...] = jnp.zeros_like(grad_hid)
 
     @pl.loop(0, 3)
     def _(a):
         cols = pl.ds(pl.multiple_of(a * heads, LANES), heads)
         made = dot_first(d_packed[:, cols], vm.a_one[...]).astype(BF16)
         grads[2 * ffn_blocks + 1 + a] = made.reshape(grads.shape[1:])
+
+
+    @pl.when(is_dec)
+    def _():
+        red.launch(2 * ffn_blocks + 1)
+        red.launch(2 * ffn_blocks + 2)
+
+    red.step(now)
+    grad_hid[...] = jnp.zeros_like(grad_hid)
+
+    @pl.loop(0, 3)
+    def _(a):
+        cols = pl.ds(pl.multiple_of(a * heads, LANES), heads)
         grad_hid[...] += dot_plain(d_packed[:, cols], vm.w_qkv[cols, :])
-
-    red.step(now + 3)
 
 
     def lower_two(rows, kept):
@@ -905,6 +954,7 @@
     small_zero = jnp.zeros((8, heads), F32)
     q_sum, v_sum = row_tiles(tokens, lower_two, (small_zero, small_zero))
     part_copy(1).start()
+    pl.when(is_enc)(lambda: red.step(now + 1))
     smalls[8:9, :] = jnp.concatenate(
         [jnp.sum(q_sum, axis=0, keepdims=True), jnp.sum(v_sum, axis=0, keepdims=True)], axis=1
     )
@@ -927,7 +977,6 @@
         return kept
 
     row_tiles(quarter, own_copy, 0)
-    red.step(now + 4)
 
     small_line = pltpu.make_async_remote_copy(
         src_ref=smalls,
@@ -975,20 +1024,21 @@
     for away in range(1, 4):
         small_pair(z, away).start()
 
-    red.far_before(now + 5)
-    red.drain(now + 5)
-    red.close()
-    pl.when(is_dec)(twin_copy().start)
-
     for away in range(1, 4):
         small_pair(lax.rem(z + 4 - away, 4), away).wait_recv()
     small_out[core] = ((small_all[0] + small_all[1]) + small_all[2]) + small_all[3]
     small_core(core).start()
+    red.far_before(now + 2 - tower)
+    red.drain(now + 2 - tower)
+    red.close()
+    pl.when(is_dec)(twin_copy().start)
+
     for away in range(1, 4):
         small_pair(z, away).wait_send()
 
     @pl.when(moved)
     def _():
+        home_move(tower_rows, tower_out, 0).wait()
         home_move(own_grad, grad_out, 1).wait()
 
     @pl.when(stays)
@@ -1001,7 +1051,7 @@
     small_core(1 - core).wait_recv()
 
 
-def tail(values, cross_grad, scale):
+def tail(values, cross_grad, tower_rows, scale):
     tokens, width = values.base.shape
     heads = values.mixed.shape[1]
     pairs = heads // LANES
@@ -1010,7 +1060,7 @@
     half = width // 2
     rows_of = heads // 2
     blocks = 2 * (width // rows_of) + 4
-    assert hidden == 2 * width and cross_grad.shape[0] == width // rows_of
+    assert hidden == 2 * width and cross_grad.shape[0] == 2
     hbm = pl.BlockSpec(memory_space=pltpu.HBM)
     vmem = pl.BlockSpec(memory_space=pltpu.VMEM)
     n_in = len(values)
@@ -1040,18 +1090,19 @@
         jax.ShapeDtypeStruct((2,) + values.smalls.shape, F32),
         jax.ShapeDtypeStruct((quarter, width), BF16),
         jax.ShapeDtypeStruct((2, heads // 2, half), BF16),
+        jax.ShapeDtypeStruct((quarter, width), BF16),
     ]
     return pl.pallas_call(
         functools.partial(tail_kernel, pairs, scale),
-        in_specs=[hbm] * (n_in + 1),
-        out_specs=[vmem] * 2 + [hbm] * 2,
+        in_specs=[hbm] * (n_in + 2),
+        out_specs=[vmem] * 2 + [hbm] * 3,
         out_shape=out_shape,
         scratch_shapes=scratch,
         compiler_params=pltpu.CompilerParams(
             collective_id=1, has_side_effects=True, vmem_limit_bytes=TAIL_LIMIT
         ),
         name="tail",
-    )(*values, cross_grad)
+    )(*values, cross_grad, tower_rows)
 
 
 class Head(NamedTuple):
@@ -1421,7 +1472,7 @@
     grad_hid, raw, grad_pre, g_low, mix_grad, dq, dkv, sum_q = (next(it) for _ in range(8))
     keys, vals, dk, dv = kv.at[0], kv.at[1], dkv.at[0], dkv.at[1]
     cot, part_send, part_recv, halves, half_near, sums, image_grad, own_rows = (next(it) for _ in range(8))
-    grads, cross_grad, near, far = (next(it) for _ in range(4))
+    grads, near, far = (next(it) for _ in range(3))
     red_sems = [next(it) for _ in range(6)]
     load_sem, store_sem, part_sem, twin_sem, side_sem, core_sem, half_sem, sum_sem, back_sem, give_sem, home_sem = it
     tower, dp, z, core, line, other, partner = spots()
@@ -1504,15 +1555,7 @@
             {DP: partner},
         )
 
-    def home_move():
-        return remote(own_rows, tower_out, home_sem.at[0], home_sem.at[1], home)
-
-    def home_stay():
-        return pltpu.make_async_copy(own_rows, tower_out, home_sem.at[0])
-
-    def go_home():
-        pl.when(moved)(home_move().start)
-        pl.when(stays)(home_stay().start)
+    rows_copy = pltpu.make_async_copy(own_rows, tower_out, home_sem.at[0])
 
     def back_copy(i):
         rows = pl.ds(i * chunk, chunk)
@@ -1527,8 +1570,9 @@
     store_grad = pltpu.make_async_copy(y2, upstream, store_sem.at[0])
     store_three = pltpu.make_async_copy(raw, d_three, store_sem.at[1])
     zero = jnp.zeros((8, width), F32)
-    blocks, rows_of = grads.shape[0], grads.shape[2]
-    red = Reducer(grads, near, far, outs, red_sems, 4, 0, blocks)
+    blocks, rows_of = outs.shape[0], outs.shape[1]
+    ffn_blocks = width // rows_of
+    red = Reducer(grads, near, far, outs, red_sems, 4, 0, blocks, blocks + 2)
 
     @pl.when(is_enc)
     def _():
@@ -1543,7 +1587,7 @@
             return kept
 
         row_tiles(quarter, lower, 0)
-        go_home()
+        rows_copy.start()
         token_relay(0)
         token_finish(0)
 
@@ -1670,7 +1714,7 @@
         @pl.loop(0, 2)
         def _(b):
             made = dot_first(grad_pre[b], act[...]).astype(BF16)
-            grads[0 : blocks // 2, b] = made.reshape(blocks // 2, rows_of, width)
+            grads[0:ffn_blocks, b] = made.reshape(ffn_blocks, rows_of, width)
 
         red.launch(0)
         red.launch(1)
@@ -1735,7 +1779,7 @@
         def _(b):
             cols = pl.ds(pl.multiple_of(b * width, LANES), width)
             made = dot_first(hid[:, cols], cot[...]).astype(BF16)
-            grads[blocks // 2 : blocks, b] = made.reshape(blocks // 2, rows_of, width)
+            grads[ffn_blocks : 2 * ffn_blocks, b] = made.reshape(ffn_blocks, rows_of, width)
 
         red.launch(4)
         red.launch(5)
@@ -1754,8 +1798,9 @@
             back_copy(i).start()
 
         half_part(3, lambda rows: dot_plain(dq[rows, :], w_cross[2].reshape(heads, width)))
-        red.add_mid(0)
-        red.step(2)
+        red.hop(0)
+        red.hop(1)
+        red.step(2, 0)
 
         def keep_two(rows, kept):
             y1[rows, :] = raw[rows, :]
@@ -1780,18 +1825,20 @@
             rows = pl.ds(h * quarter, quarter)
             part_send[1, rows, :] = pre[rows, :].astype(BF16)
             part_copy(1, h).start()
-        red.step(3)
+        red.add_mid(0)
+        red.step(3, 0)
+        red.add_mid(1)
+        grads[2 * ffn_blocks] = dot_first(dq[...], act_txt[...]).astype(BF16).reshape(grads.shape[1:])
+        grads[2 * ffn_blocks + 1] = dot_first(mixed[...], g_low[...]).astype(BF16).reshape(grads.shape[1:])
+        red.add_mid(2)
+        red.step(4)
 
         @pl.loop(0, 2)
         def _(which):
             made = dot_first(dkv[which, 0], images[0]) + dot_first(dkv[which, 1], images[1])
-            cross_grad[which] = made.astype(BF16).reshape(cross_grad.shape[1:])
-
-        red.step(4)
-        cross_grad[2] = dot_first(dq[...], act_txt[...]).astype(BF16).reshape(cross_grad.shape[1:])
-        cross_grad[3] = dot_first(mixed[...], g_low[...]).astype(BF16).reshape(cross_grad.shape[1:])
-        store_cross = pltpu.make_async_copy(cross_grad, cross_out, store_sem.at[2])
-        store_cross.start()
+            grads[blocks + which] = made.astype(BF16).reshape(grads.shape[1:])
+
+        red.step(5)
         for h in range(2):
             part_copy(1, h).wait()
 
@@ -1802,9 +1849,11 @@
             return kept
 
         row_tiles(quarter, add_last, 0)
-        go_home()
-        red.far_before(5)
-        red.drain(5)
+        rows_copy.start()
+        red.far_before(6)
+        red.drain(6)
+        store_cross = pltpu.make_async_copy(near.at[pl.ds(blocks, 2)], cross_out, store_sem.at[2])
+        store_cross.start()
         red.close()
         store_cross.wait()
         for i in range(CHUNKS):
@@ -1818,8 +1867,7 @@
         for k in range(len(pieces)):
             sent(k)
 
-    pl.when(moved)(home_move().wait)
-    pl.when(stays)(home_stay().wait)
+    rows_copy.wait()
     store_grad.wait()
     store_three.wait()
 
@@ -1834,9 +1882,9 @@
     chunk = quarter // CHUNKS
     assert chunk * CHUNKS == quarter
     rows_of = heads // 2
-    blocks = 2 * (width // rows_of)
+    blocks = 2 * (width // rows_of) + 2
     assert hidden == 2 * width
-    cross_shape = (4, 2, rows_of, width)
+    cross_shape = (2, 2, rows_of, half)
     rows = ffn_shard.shape[1]
     pieces = [(0, 0, 0, 1, at, rows // 4, 1, False) for at in range(rows // 2, rows, rows // 4)]
     n = len(pieces)
@@ -1878,9 +1926,9 @@
         pltpu.VMEM(low, BF16),
         pltpu.VMEM((quarter, width), BF16),
     ]
-    scratch += [pltpu.VMEM((blocks, 2, rows_of, width), BF16), pltpu.VMEM(cross_shape, BF16)]
-    scratch += [pltpu.VMEM((blocks, 2, rows_of, half), BF16)] * 2
-    scratch += [dma((blocks,)), dma((blocks,)), dma((blocks, 2)), dma((blocks, 2)), dma((blocks,)), dma((blocks,))]
+    scratch += [pltpu.VMEM((blocks + 2, 2, rows_of, width), BF16), pltpu.VMEM((blocks + 2, 2, rows_of, half), BF16)]
+    scratch += [pltpu.VMEM((blocks, 2, rows_of, half), BF16)]
+    scratch += [dma((blocks + 2,)), dma((blocks + 2,)), dma((blocks, 2)), dma((blocks, 2)), dma((blocks,)), dma((blocks,))]
     scratch += [
         dma((6,)),
         dma((3,)),
@@ -1940,7 +1988,7 @@
     bring(1, late.at[pl.ds(0, n)], early.at[pl.ds(n, n)], b_mlp)
     bring(2, late.at[2 * n], late.at[2 * n], b_out)
     bring(3, late.at[pl.ds(2 * n + 1, 3)], late.at[pl.ds(2 * n + 1, 3)], b_qkv)
-    bring(4, from_text, late.at[pl.ds(n + 2, 2)], b_cross)
+    bring(4, from_text, early.at[pl.ds(2 * n, 2)], b_cross)
     for i in range(2):
         pltpu.make_async_copy(rows_in[i], held[i], sem.at[5 + i]).start()
 
@@ -1996,7 +2044,7 @@
     struct = jax.ShapeDtypeStruct
     width = total.shape[2]
     blocks, cols, half = early.shape
-    n = blocks // 2
+    n = (blocks - 2) // 2
     ffn, cut = n * cols, half // 2
     out_shape = [struct((1,) + x.shape, BF16) for x in token_rows]
     out_shape += [
@@ -2221,7 +2269,7 @@
         cross_q = dot_rows(act_three, w_cross[2]).astype(BF16)
 
     if direct:
-        back_in_three, upstream, smalls, tower_out, g_cross, early = middle(
+        back_in_three, upstream, smalls, tower_rows, g_cross, early = middle(
             first, gathered[2], gathered[3], gathered[4], mlp_out, out_cot[0], vecs, picks, scale_qk
         )
         values = Tail(
@@ -2246,7 +2294,7 @@
             w_qkv=w_qkv,
             x0=stream_low,
         )
-        late, total, grad_in, from_text = tail(values, g_cross, scale_qk)
+        late, total, grad_in, from_text, tower_out = tail(values, g_cross, tower_rows, scale_qk)
         return finish(late, early, from_text, total, [tower_out, grad_in])
     else:
         near_half = lax.ppermute(own_rows(act_three), TOWER, [(0, 1)])

time: 340 us -> 331 us (0.974)
  Pallas kernels: 335 us -> 327 us
    pallas_call x1, Pallas kernels: 84.9 us -> 73.6 us  [tail(): pl.pallas_call(functools.partial(tail_kernel, pairs, scale), in_specs=[hb...]
where the time goes in v1:
time: 331 us; the launch traced here: 328 us
  Pallas kernels  327 us (99%)
    pallas_call x1, Pallas kernels, middle(): pl.pallas_call(functools.partial(mid_kernel, tuple(pieces), pairs, scale)...  151 us
    pallas_call x1, Pallas kernels, head(): pl.pallas_call(functools.partial(head_kernel, tuple(pieces), pairs, scale...  96 us
    pallas_call x1, Pallas kernels, tail(): pl.pallas_call(functools.partial(tail_kernel, pairs, scale), in_specs=[hb...  73.6 us

profile of v1, /device:TPU:11, one launch (start us, length us, event | category | flops | bytes accessed | tf_op | source)
XLA Modules:
  0.0 327.6 jit_solution(2256440493529936319)
XLA Ops:
  0.6 96.0 %head.1 = (bf16[3,2,192,768]{3,2,1,0:T(8,128)(2,1)}, bf16[1,2,192,768]{3,2,1,0:T(8,128)(2,1)}, bf16[4,2,192,768]{3,2,1,0:T(8,128)(2,1)}, bf16[1,2,768,768]{3,2,1...) custom-call(bf16[3,192,768]{2,1,0:T(8,128)(2,1)} %bitcast.21, ...), custom_call_target="tpu_custom_call" | custom-call | tf_op jit(solution)/shard_map/head/pallas_call | solution.py:1443
  96.7 151.5 %middle.1 = (f32[576,768]{1,0:T(8,128)}, f32[576,768]{1,0:T(8,128)}, f32[16,768]{1,0:T(8,128)}, bf16[288,768]{1,0:T(8,128)(2,1)}, bf16[2,2,192,384]{3,2,1,0:T(8,128)(2,1)}, /*index=5*/bf16[10,192,384]{2,1,0:T(8,128)(2,1)}) custom-call(bf16[576,768]{1,0:T(8,128)(2,1)} %get-tuple-element.57.refs_0_, f32[576,768]{1,0:T(8,128)} %get-tuple-element.58.refs_1_.refs_10_, ...), custom_call_target="tpu_custom_call" | custom-call | tf_op jit(solution)/shard_map/middle/pallas_call | solution.py:1954
  248.2 73.6 %tail.1 = (bf16[12,192,384]{2,1,0:T(8,128)(2,1)}, f32[2,16,768]{2,1,0:T(8,128)}, bf16[288,768]{1,0:T(8,128)(2,1)}, bf16[2,192,384]{2,1,0:T(8,128)(2,1)}, bf16[288,768]{1,0:T(8,128)(2,1)}) custom-call(f32[576,768]{1,0:T(8,128)} %get-tuple-element.65.refs_0_, f32[576,768]{1,0:T(8,128)} %get-tuple-element.63.refs_8_.refs_1_, ...), custom_call_target="tpu_custom_call" | custom-call | tf_op jit(solution)/shard_map/tail/pallas_call | solution.py:1095
  321.8 5.6 %finish.1 = (bf16[1,288,768]{2,1,0:T(8,128)(2,1)}, bf16[1,288,768]{2,1,0:T(8,128)(2,1)}, f32[1,3,192,192]{3,2,1,0:T(8,128)}, f32[1,192,192]{2,1,0:T(8,128)}, f32...) custom-call(bf16[12,192,384]{2,1,0:T(8,128)(2,1)} %get-tuple-element, ...), custom_call_target="tpu_custom_call" | custom-call | tf_op jit(solution)/shard_map/finish/pallas_call | solution.py:2066

commit v2 on v1

--- a/solution.py
+++ b/solution.py
@@ -74,7 +74,7 @@
     pl.semaphore_signal(pltpu.get_barrier_semaphore(), inc=1, device_id=target, device_id_type=MESH)
 
 
-def weight_steps(pieces, srcs, outs, stages, sems):
+def weight_steps(pieces, srcs, outs, stages, sems, less):
     send_sem, recv_sem, local_sem, twin_send, twin_recv = sems
     tower, dp, z, core, line, other, partner = spots()
     place = z + core * (3 - 2 * z)
@@ -129,30 +129,34 @@
     def gate(piece, cond):
         return cond if piece[6] is None else jnp.logical_and(cond, tower == piece[6])
 
-    def send_own(k):
+    def send_own(k, seat):
         piece = pieces[k]
 
-        @pl.when(gate(piece, place == 0))
-        def _():
-            move(k, own(piece), slot_of[0], line, 0, 0, {MP: ahead}).start()
-
-        @pl.when(gate(piece, place == 1))
-        def _():
-            move(k, own(piece), slot_of[1], line, 1, 1, {MP: ahead}).start()
-            move(k, own(piece), slot_of[1], line, 2, 1, {MP: behind}).start()
+        if seat == 0:
+
+            @pl.when(gate(piece, place == 0))
+            def _():
+                move(k, own(piece), slot_of[0], line, 0, 0, {MP: ahead}).start()
+
+        else:
+
+            @pl.when(gate(piece, place == 1))
+            def _():
+                move(k, own(piece), slot_of[1], line, 1, 1, {MP: ahead}).start()
+                move(k, own(piece), slot_of[1], line, 2, 1, {MP: behind}).start()
 
     orders = {t: [k for k, p in enumerate(pieces) if p[6] in (None, t)] for t in (0, 1)}
 
-    def launch(t, place):
-        if place >= len(orders[t]):
+    def launch(t, at, seat):
+        if at >= len(orders[t]):
             return
-        k = orders[t][place]
-
-        @pl.when(jnp.logical_and(holder, tower == t))
+        k = orders[t][at]
+
+        @pl.when(jnp.logical_and(place == seat, tower == t))
         def _():
             if far_src and k == far_src[0]:
                 twin_copy().wait_recv()
-            send_own(k)
+            send_own(k, seat)
 
     def own_sent(k):
         piece = pieces[k]
@@ -174,8 +178,9 @@
                 twin_copy().start()
 
         for t in (0, 1):
-            for start in range(WINDOW):
-                launch(t, start)
+            for seat in (0, 1):
+                for start in range(WINDOW - less * seat):
+                    launch(t, start, seat)
 
     def keeps(i):
         flags = {p[6] for p in pieces if p[0] == i}
@@ -224,7 +229,8 @@
         own_sent(k)
         for t in (0, 1):
             if k in orders[t]:
-                launch(t, orders[t].index(k) + WINDOW)
+                for seat in (0, 1):
+                    launch(t, orders[t].index(k) + WINDOW - less * seat, seat)
 
     def arrived(k):
         piece = pieces[k]
@@ -666,6 +672,8 @@
 
 
 class Tail(NamedTuple):
+    seg_col: Any
+    seg_row: Any
     d_three: Any
     base: Any
     upstream: Any
@@ -681,14 +689,12 @@
     mixed: Any
     packed: Any
     tops: Any
-    seg_col: Any
-    seg_row: Any
     a_one: Any
     w_qkv: Any
     x0: Any
 
 
-IMAGE_ONLY = Tail._fields[5:11]
+IMAGE_ONLY = Tail._fields[7:13]
 
 
 def tail_kernel(pairs, scale, *refs):
@@ -802,6 +808,8 @@
         )
 
     zero = jnp.zeros((8, width), F32)
+    need(vm.seg_col, vm.seg_row)
+    fill_mask(mask, vm.seg_col, vm.seg_row, is_dec)
     need(vm.d_three, vm.base, vm.upstream, vm.gains, vm.smalls)
     smalls[...] = vm.smalls[...]
 
@@ -888,11 +896,10 @@
     def _():
         put(0, bias)
 
-    need(vm.w_out, vm.mixed, vm.packed, vm.tops, vm.seg_col, vm.seg_row)
+    need(vm.w_out, vm.mixed, vm.packed, vm.tops)
     mix_grad[...] = dot_rows(g_low[...], vm.w_out[...]).astype(BF16)
     grads[2 * ffn_blocks] = dot_first(vm.mixed[...], g_low[...]).astype(BF16).reshape(grads.shape[1:])
 
-    fill_mask(mask, vm.seg_col, vm.seg_row, is_dec)
 
     @pl.when(is_enc)
     def _():
@@ -1017,6 +1024,8 @@
             device_id_type=MESH,
         )
 
+    after = now + 2 - tower
+    red.step(after)
     small_line.wait()
     small_all[z] = smalls[...] + small_near[...]
 
@@ -1024,12 +1033,13 @@
     for away in range(1, 4):
         small_pair(z, away).start()
 
+    red.step(after + 1)
     for away in range(1, 4):
         small_pair(lax.rem(z + 4 - away, 4), away).wait_recv()
     small_out[core] = ((small_all[0] + small_all[1]) + small_all[2]) + small_all[3]
     small_core(core).start()
-    red.far_before(now + 2 - tower)
-    red.drain(now + 2 - tower)
+    red.far_before(after + 2)
+    red.drain(after + 2)
     red.close()
     pl.when(is_dec)(twin_copy().start)
 
@@ -1159,7 +1169,7 @@
     )
 
     begin, begin_local, pass_on, arrived, sent, end_local, end_twin = weight_steps(
-        pieces, srcs, outs, stages, weight_sems
+        pieces, srcs, outs, stages, weight_sems, 1
     )
     token_begin, token_relay, token_finish = token_steps(blocks, tokens, token_stage, token_sems)
     token_begin(0)
@@ -1213,6 +1223,17 @@
             device_id_type=MESH,
         )
 
+    def last_copy(i):
+        rows = pl.ds(pl.multiple_of(i * (count // 2), 32), count // 2)
+        return pltpu.make_async_remote_copy(
+            src_ref=part_send.at[1, rows, :],
+            dst_ref=part_recv.at[1, rows, :],
+            send_sem=part_sem.at[1 + i, 0],
+            recv_sem=part_sem.at[1 + i, 1],
+            device_id={DP: partner},
+            device_id_type=MESH,
+        )
+
     def normed(source, target, which):
         gain, shift = gains[which], shifts[which]
 
@@ -1321,22 +1342,52 @@
         relay(1)
         store(vm.pre).start()
         store(vm.hid).start()
+        cut = width // 2
+        raw[...] = jnp.zeros_like(raw)
+        end_local(4)
+
+        def half_load(i):
+            rows = pl.ds(i * cut, cut)
+            return load(4, w_mlp.at[:, :, rows, :], outs[4].at[:, :, rows, :])
+
+        for k in enc_mlp[:2]:
+            arrived(k)
+        half_load(0).start()
         relay(len(waiting[0]))
-        for k in enc_mlp:
+        half_load(0).wait()
+
+        @pl.loop(0, 2)
+        def _(b):
+            raw[...] += dot_plain(vm.hid[:, pl.ds(pl.multiple_of(b * width, LANES), cut)], w_mlp[0, b, 0:cut, :])
+
+        for k in enc_mlp[2:]:
             arrived(k)
-        end_local(4)
-        load(4, w_mlp, outs[4]).start()
-        load(4, w_mlp, outs[4]).wait()
-        part_send[1] = dot_plain(vm.hid[...], w_mlp[0].reshape(2 * width, width)).astype(BF16)
-        part_copy(1).start()
-        part_copy(1).wait()
+        half_load(1).start()
+        half_load(1).wait()
+        half = count // 2
+
+        @pl.loop(0, 2)
+        def _(i):
+            rows = pl.ds(pl.multiple_of(i * half, 32), half)
+            made = raw[rows, :]
+            for b in range(2):
+                made = made + dot_plain(vm.hid[rows, pl.ds(b * width + cut, cut)], w_mlp[0, b, cut:width, :])
+            part_send[1, rows, :] = made.astype(BF16)
+            last_copy(i).start()
 
         def add_two(rows, kept):
             total = part_send[1, rows, :].astype(F32) + part_recv[1, rows, :].astype(F32)
-            vm.base[rows, :] = vm.x1[rows, :] + total + ffn_out_b[...]
+            value = vm.x1[rows, :] + total + ffn_out_b[...]
+            vm.base[rows, :] = value
+            unit, _ = norm_parts(value)
+            vm.act_three[rows, :] = (unit * gains[2] + shifts[2]).astype(BF16)
             return kept
 
-        row_tiles(count, add_two, 0)
+        @pl.loop(0, 2)
+        def _(i):
+            last_copy(i).wait()
+            row_tiles(half, add_two, 0, i * half)
+
 
     @pl.when(is_dec)
     def _():
@@ -1345,10 +1396,10 @@
             return kept
 
         row_tiles(count, same, 0)
-
+        normed(vm.base, vm.act_three, 2)
+
+    store(vm.act_three).start()
     store(vm.base).start()
-    normed(vm.base, vm.act_three, 2)
-    store(vm.act_three).start()
 
     @pl.when(is_dec)
     def _():
@@ -1438,7 +1489,7 @@
         dma((3, 2)),
         dma((5,)),
         dma((len(made),)),
-        dma((2, 2)),
+        dma((3, 2)),
     ]
     results = pl.pallas_call(
         functools.partial(head_kernel, tuple(pieces), pairs, scale),
@@ -1529,7 +1580,7 @@
     token_begin, token_relay, token_finish = token_steps([cot_block], [cot], token_stage, token_sems)
     pl.when(is_enc)(functools.partial(token_begin, 0))
     begin, begin_local, pass_on, arrived, sent, end_local, _ = weight_steps(
-        pieces, [ffn_shard], [w_mlp], stages, weight_sems
+        pieces, [ffn_shard], [w_mlp], stages, weight_sems, 0
     )
 
     def load(i, source, target):
@@ -1546,7 +1597,7 @@
     ]
 
     def part_copy(k, h):
-        rows = pl.ds(h * quarter, quarter)
+        rows = pl.ds(pl.multiple_of(h * quarter, 32), quarter)
         return remote(
             part_send.at[k % 3, rows, :],
             part_recv.at[k % 3, rows, :],
@@ -1615,6 +1666,7 @@
 
     @pl.when(is_dec)
     def _():
+        begin()
         for one in early + text_loads:
             one.start()
         for one in early:
@@ -1629,7 +1681,8 @@
             twin_copy(i).wait_recv()
             side_copy(i, side).start()
             core_copy(i, side, core, 0).start()
-        begin()
+        for k in range(len(pieces)):
+            pass_on(k)
         for one in text_loads[:2]:
             one.wait()
         mixed[...] = jnp.zeros_like(mixed)
@@ -1655,20 +1708,21 @@
 
             cross_forward(image, query, keys, vals, picks, mixed, tops, pairs, scale)
 
-        for k in range(len(pieces)):
-            pass_on(k)
         token_relay(0)
 
         def half_part(k, made):
-            for h in range(2):
-                part_send[k % 3, pl.ds(h * quarter, quarter), :] = made(pl.ds(h * quarter, quarter)).astype(BF16)
+            @pl.loop(0, 2)
+            def _(h):
+                rows = pl.ds(pl.multiple_of(h * quarter, 32), quarter)
+                part_send[k % 3, rows, :] = made(rows).astype(BF16)
                 part_copy(k, h).start()
 
         def add_halves(k, run, carry):
-            for h in range(2):
+            def half(h, kept):
                 part_copy(k, h).wait()
-                carry = row_tiles(quarter, run, carry, h * quarter)
-            return carry
+                return row_tiles(quarter, run, kept, h * quarter)
+
+            return lax.fori_loop(0, 2, half, carry)
 
         half_part(0, lambda rows: dot_plain(mixed[rows, :], w_cross[3].reshape(heads, width)))
         for one in text_loads[2:]:

time: 331 us -> 323 us (0.976)
  Pallas kernels: 327 us -> 319 us
    pallas_call x1, Pallas kernels: 73.6 us -> 66.7 us  [tail(): pl.pallas_call(functools.partial(tail_kernel, pairs, scale), in_specs=[hb...]
where the time goes in v2:
time: 323 us; the launch traced here: 319 us
  Pallas kernels  319 us (99%)
    pallas_call x1, Pallas kernels, middle(): pl.pallas_call(functools.partial(mid_kernel, tuple(pieces), pairs, scale)...  151 us
    pallas_call x1, Pallas kernels, head(): pl.pallas_call(functools.partial(head_kernel, tuple(pieces), pairs, scale...  94.8 us
    pallas_call x1, Pallas kernels, tail(): pl.pallas_call(functools.partial(tail_kernel, pairs, scale), in_specs=[hb...  66.7 us

profile of v2, /device:TPU:11, one launch (start us, length us, event | category | flops | bytes accessed | tf_op | source)
XLA Modules:
  0.0 319.4 jit_solution(10495436737318292723)
XLA Ops:
  0.6 94.8 %head.1 = (bf16[3,2,192,768]{3,2,1,0:T(8,128)(2,1)}, bf16[1,2,192,768]{3,2,1,0:T(8,128)(2,1)}, bf16[4,2,192,768]{3,2,1,0:T(8,128)(2,1)}, bf16[1,2,768,768]{3,2,1...) custom-call(bf16[3,192,768]{2,1,0:T(8,128)(2,1)} %bitcast.21, ...), custom_call_target="tpu_custom_call" | custom-call | tf_op jit(solution)/shard_map/head/pallas_call | solution.py:1494
  95.5 151.5 %middle.1 = (f32[576,768]{1,0:T(8,128)}, f32[576,768]{1,0:T(8,128)}, f32[16,768]{1,0:T(8,128)}, bf16[288,768]{1,0:T(8,128)(2,1)}, bf16[2,2,192,384]{3,2,1,0:T(8,128)(2,1)}, /*index=5*/bf16[10,192,384]{2,1,0:T(8,128)(2,1)}) custom-call(bf16[576,768]{1,0:T(8,128)(2,1)} %get-tuple-element.59.refs_0_, f32[576,768]{1,0:T(8,128)} %get-tuple-element.60.refs_1_.refs_12_, ...), custom_call_target="tpu_custom_call" | custom-call | tf_op jit(solution)/shard_map/middle/pallas_call | solution.py:2008
  247.0 66.7 %tail.1 = (bf16[12,192,384]{2,1,0:T(8,128)(2,1)}, f32[2,16,768]{2,1,0:T(8,128)}, bf16[288,768]{1,0:T(8,128)(2,1)}, bf16[2,192,384]{2,1,0:T(8,128)(2,1)}, bf16[288,768]{1,0:T(8,128)(2,1)}) custom-call(s32[576,128]{1,0:T(8,128)} %get-tuple-element.57.refs_0_, s32[8,576]{1,0:T(8,128)} %get-tuple-element.58.refs_1_, f32[576,768]{1,0:T(8,128)} %get-tuple-element.67.refs_2_, ...), custom_call_target="tpu_custom_call" | custom-call | tf_op jit(solution)/shard_map/tail/pallas_call | solution.py:1105
  313.7 5.6 %finish.1 = (bf16[1,288,768]{2,1,0:T(8,128)(2,1)}, bf16[1,288,768]{2,1,0:T(8,128)(2,1)}, f32[1,3,192,192]{3,2,1,0:T(8,128)}, f32[1,192,192]{2,1,0:T(8,128)}, f32...) custom-call(bf16[12,192,384]{2,1,0:T(8,128)(2,1)} %get-tuple-element, ...), custom_call_target="tpu_custom_call" | custom-call | tf_op jit(solution)/shard_map/finish/pallas_call | solution.py:2120

commit v3 on v2

--- a/solution.py
+++ b/solution.py
@@ -651,7 +651,7 @@
         def _(k):
             self.add_far(k)
 
-    def close(self):
+    def close(self, got):
         @pl.loop(self.first, self.last)
         def _(k):
             pl.when(self.place == 3)(self.inward(k).wait_send)
@@ -666,7 +666,7 @@
                 self.beside(k).wait_send()
                 self.to_core(k).wait_send()
 
-            @pl.when(jnp.logical_not(self.holder))
+            @pl.when(jnp.logical_and(jnp.logical_not(self.holder), k >= got))
             def _():
                 self.to_core(k).wait_recv()
 
@@ -726,6 +726,19 @@
     peers = [(None, {DP: other}), (None, {DP: partner}), (is_enc, {TOWER: 1 - tower})]
     peers += [(None, {MP: lax.rem(z + away, 4)}) for away in range(1, 4)]
     peers += [(moved, home), (moved, guest)]
+    def load(i):
+        return pltpu.make_async_copy(hbm[i], vm[i], load_sem.at[i])
+
+    def on_side(i, run):
+        if Tail._fields[i] in IMAGE_ONLY:
+            pl.when(is_enc)(run)
+        else:
+            run()
+
+    pl.when(is_dec)(lambda: pltpu.make_async_copy(cross_in, near.at[pl.ds(text_first, 2)], load_sem.at[len(hbm)]).start())
+    for i in range(len(hbm)):
+        on_side(i, load(i).start)
+
     barrier_all(
         peers,
         [
@@ -736,19 +749,6 @@
         ],
     )
 
-    def load(i):
-        return pltpu.make_async_copy(hbm[i], vm[i], load_sem.at[i])
-
-    def on_side(i, run):
-        if Tail._fields[i] in IMAGE_ONLY:
-            pl.when(is_enc)(run)
-        else:
-            run()
-
-    pl.when(is_dec)(lambda: pltpu.make_async_copy(cross_in, near.at[pl.ds(text_first, 2)], load_sem.at[len(hbm)]).start())
-    for i in range(len(hbm)):
-        on_side(i, load(i).start)
-
     def need(*wanted):
         for i, ref in enumerate(vm):
             if any(ref is one for one in wanted):
@@ -756,7 +756,7 @@
 
     first_block = text_first * tower
     blocks = grads.shape[0]
-    red = Reducer(grads, near, far, outs, red_sems, 2 + tower, first_block, blocks, blocks)
+    red = Reducer(grads, near, far, outs, red_sems, 2 + 2 * tower, first_block, blocks, blocks)
 
     def twin_copy():
         return pltpu.make_async_remote_copy(
@@ -935,12 +935,7 @@
         cols = pl.ds(pl.multiple_of(a * heads, LANES), heads)
         made = dot_first(d_packed[:, cols], vm.a_one[...]).astype(BF16)
         grads[2 * ffn_blocks + 1 + a] = made.reshape(grads.shape[1:])
-
-
-    @pl.when(is_dec)
-    def _():
-        red.launch(2 * ffn_blocks + 1)
-        red.launch(2 * ffn_blocks + 2)
+        pl.when(is_dec)(lambda: red.launch(2 * ffn_blocks + 1 + a))
 
     red.step(now)
     grad_hid[...] = jnp.zeros_like(grad_hid)
@@ -1039,9 +1034,18 @@
     small_out[core] = ((small_all[0] + small_all[1]) + small_all[2]) + small_all[3]
     small_core(core).start()
     red.far_before(after + 2)
+
+    @pl.when(is_dec)
+    def _():
+        @pl.when(jnp.logical_not(red.holder))
+        def _():
+            for k in range(2):
+                red.to_core(text_first + k).wait_recv()
+
+        twin_copy().start()
+
     red.drain(after + 2)
-    red.close()
-    pl.when(is_dec)(twin_copy().start)
+    red.close((text_first + 2) * tower)
 
     for away in range(1, 4):
         small_pair(z, away).wait_send()
@@ -1908,7 +1912,7 @@
         red.drain(6)
         store_cross = pltpu.make_async_copy(near.at[pl.ds(blocks, 2)], cross_out, store_sem.at[2])
         store_cross.start()
-        red.close()
+        red.close(0)
         store_cross.wait()
         for i in range(CHUNKS):
             side_copy(i, side).wait_send()

time: 323 us -> 312 us (0.966)
  Pallas kernels: 319 us -> 310 us
    pallas_call x1, Pallas kernels: 66.7 us -> 58.5 us  [tail(): pl.pallas_call(functools.partial(tail_kernel, pairs, scale), in_specs=[hb...]
where the time goes in v3:
time: 312 us; the launch traced here: 311 us
  Pallas kernels  310 us (99%)
    pallas_call x1, Pallas kernels, middle(): pl.pallas_call(functools.partial(mid_kernel, tuple(pieces), pairs, scale)...  151 us
    pallas_call x1, Pallas kernels, head(): pl.pallas_call(functools.partial(head_kernel, tuple(pieces), pairs, scale...  94.8 us
    pallas_call x1, Pallas kernels, tail(): pl.pallas_call(functools.partial(tail_kernel, pairs, scale), in_specs=[hb...  58.5 us

profile of v3, /device:TPU:11, one launch (start us, length us, event | category | flops | bytes accessed | tf_op | source)
XLA Modules:
  0.0 311.2 jit_solution(1070199281280107838)
XLA Ops:
  0.6 94.8 %head.1 = (bf16[3,2,192,768]{3,2,1,0:T(8,128)(2,1)}, bf16[1,2,192,768]{3,2,1,0:T(8,128)(2,1)}, bf16[4,2,192,768]{3,2,1,0:T(8,128)(2,1)}, bf16[1,2,768,768]{3,2,1...) custom-call(bf16[3,192,768]{2,1,0:T(8,128)(2,1)} %bitcast.21, ...), custom_call_target="tpu_custom_call" | custom-call | tf_op jit(solution)/shard_map/head/pallas_call | solution.py:1498
  95.5 151.5 %middle.1 = (f32[576,768]{1,0:T(8,128)}, f32[576,768]{1,0:T(8,128)}, f32[16,768]{1,0:T(8,128)}, bf16[288,768]{1,0:T(8,128)(2,1)}, bf16[2,2,192,384]{3,2,1,0:T(8,128)(2,1)}, /*index=5*/bf16[10,192,384]{2,1,0:T(8,128)(2,1)}) custom-call(bf16[576,768]{1,0:T(8,128)(2,1)} %get-tuple-element.59.refs_0_, f32[576,768]{1,0:T(8,128)} %get-tuple-element.60.refs_1_.refs_12_, ...), custom_call_target="tpu_custom_call" | custom-call | tf_op jit(solution)/shard_map/middle/pallas_call | solution.py:2012
  247.0 58.5 %tail.1 = (bf16[12,192,384]{2,1,0:T(8,128)(2,1)}, f32[2,16,768]{2,1,0:T(8,128)}, bf16[288,768]{1,0:T(8,128)(2,1)}, bf16[2,192,384]{2,1,0:T(8,128)(2,1)}, bf16[288,768]{1,0:T(8,128)(2,1)}) custom-call(s32[576,128]{1,0:T(8,128)} %get-tuple-element.57.refs_0_, s32[8,576]{1,0:T(8,128)} %get-tuple-element.58.refs_1_, f32[576,768]{1,0:T(8,128)} %get-tuple-element.67.refs_2_, ...), custom_call_target="tpu_custom_call" | custom-call | tf_op jit(solution)/shard_map/tail/pallas_call | solution.py:1109
  305.4 5.6 %finish.1 = (bf16[1,288,768]{2,1,0:T(8,128)(2,1)}, bf16[1,288,768]{2,1,0:T(8,128)(2,1)}, f32[1,3,192,192]{3,2,1,0:T(8,128)}, f32[1,192,192]{2,1,0:T(8,128)}, f32...) custom-call(bf16[12,192,384]{2,1,0:T(8,128)(2,1)} %get-tuple-element, ...), custom_call_target="tpu_custom_call" | custom-call | tf_op jit(solution)/shard_map/finish/pallas_call | solution.py:2124

commit v4 on v3

--- a/solution.py
+++ b/solution.py
@@ -1811,10 +1811,6 @@
             halves[image] = made.astype(BF16)
             half_copy(image, 1 - i).start()
 
-        for k in range(2):
-            red.add_near(k, False)
-            red.launch(k + 2)
-
         def sum_copy(i):
             rows = pl.ds(i * chunk, chunk)
             return remote(
@@ -1833,6 +1829,10 @@
 
             row_tiles(chunk, add_far, 0)
             sum_copy(i).start()
+        for k in range(2):
+            red.add_near(k, False)
+            red.launch(k + 2)
+
         @pl.loop(0, 2)
         def _(b):
             cols = pl.ds(pl.multiple_of(b * width, LANES), width)
@@ -2071,6 +2071,11 @@
         wide = block.astype(F32)
         return jnp.where(core == 0, wide[:, :cut], wide[:, cut:])
 
+    def mine_turned(block):
+        tall = block.T
+        cut = tall.shape[0] // 2
+        return jnp.where(core == 0, tall[:cut].astype(F32), tall[cut:].astype(F32))
+
     for i in range(2):
         pltpu.make_async_copy(rows_in[i], held[i], sem.at[5 + i]).wait()
         pltpu.make_async_copy(held[i], rows_out[i].at[0], sem.at[7 + i]).start()
@@ -2079,19 +2084,19 @@
     pltpu.make_async_copy(late.at[pl.ds(0, n)], b_in, sem.at[0]).wait()
     for i in range(n // 2):
         pair = b_in[2 * i : 2 * i + 2].reshape(2 * cols, half)
-        o_in[0, :, 2 * i * cols : 2 * (i + 1) * cols] = mine(pair).T
+        o_in[0, :, 2 * i * cols : 2 * (i + 1) * cols] = mine_turned(pair)
     pltpu.make_async_copy(late.at[pl.ds(0, n)], b_mlp, sem.at[1]).wait()
     for i in range(n // 2):
         pair = b_mlp[2 * i : 2 * i + 2].reshape(2 * cols, half)
-        o_mlp[0, :, 2 * i * cols : 2 * (i + 1) * cols] = mine(pair).T
+        o_mlp[0, :, 2 * i * cols : 2 * (i + 1) * cols] = mine_turned(pair)
     pltpu.make_async_copy(late.at[0], b_out, sem.at[2]).wait()
     o_out[0] = mine(b_out[...])
     pltpu.make_async_copy(late.at[pl.ds(0, 3)], b_qkv, sem.at[3]).wait()
     for a in range(3):
-        o_qkv[0, a] = mine(b_qkv[a]).T
+        o_qkv[0, a] = mine_turned(b_qkv[a])
     pltpu.make_async_copy(late.at[pl.ds(0, 2)], b_cross, sem.at[4]).wait()
     for a in range(2):
-        o_cross[0, a] = mine(b_cross[a]).T
+        o_cross[0, a] = mine_turned(b_cross[a])
     for i in range(2):
         pltpu.make_async_copy(held[i], rows_out[i].at[0], sem.at[7 + i]).wait()
 

time: 312 us -> 311 us (level)
  no operation moved by 1% of the time
where the time goes in v4:
time: 311 us
  Pallas kernels  310 us (100%)
    pallas_call x1, Pallas kernels, middle(): pl.pallas_call(functools.partial(mid_kernel, tuple(pieces), pairs, scale)...  151 us
    pallas_call x1, Pallas kernels, head(): pl.pallas_call(functools.partial(head_kernel, tuple(pieces), pairs, scale...  94.8 us
    pallas_call x1, Pallas kernels, tail(): pl.pallas_call(functools.partial(tail_kernel, pairs, scale), in_specs=[hb...  58.5 us

profile of v4, /device:TPU:11, one launch (start us, length us, event | category | flops | bytes accessed | tf_op | source)
XLA Modules:
  0.0 310.7 jit_solution(15411581538955975245)
XLA Ops:
  0.6 94.8 %head.1 = (bf16[3,2,192,768]{3,2,1,0:T(8,128)(2,1)}, bf16[1,2,192,768]{3,2,1,0:T(8,128)(2,1)}, bf16[4,2,192,768]{3,2,1,0:T(8,128)(2,1)}, bf16[1,2,768,768]{3,2,1...) custom-call(bf16[3,192,768]{2,1,0:T(8,128)(2,1)} %bitcast.21, ...), custom_call_target="tpu_custom_call" | custom-call | tf_op jit(solution)/shard_map/head/pallas_call | solution.py:1498
  95.5 151.5 %middle.1 = (f32[576,768]{1,0:T(8,128)}, f32[576,768]{1,0:T(8,128)}, f32[16,768]{1,0:T(8,128)}, bf16[288,768]{1,0:T(8,128)(2,1)}, bf16[2,2,192,384]{3,2,1,0:T(8,128)(2,1)}, /*index=5*/bf16[10,192,384]{2,1,0:T(8,128)(2,1)}) custom-call(bf16[576,768]{1,0:T(8,128)(2,1)} %get-tuple-element.59.refs_0_, f32[576,768]{1,0:T(8,128)} %get-tuple-element.60.refs_1_.refs_12_, ...), custom_call_target="tpu_custom_call" | custom-call | tf_op jit(solution)/shard_map/middle/pallas_call | solution.py:2012
  247.0 58.5 %tail.1 = (bf16[12,192,384]{2,1,0:T(8,128)(2,1)}, f32[2,16,768]{2,1,0:T(8,128)}, bf16[288,768]{1,0:T(8,128)(2,1)}, bf16[2,192,384]{2,1,0:T(8,128)(2,1)}, bf16[288,768]{1,0:T(8,128)(2,1)}) custom-call(s32[576,128]{1,0:T(8,128)} %get-tuple-element.57.refs_0_, s32[8,576]{1,0:T(8,128)} %get-tuple-element.58.refs_1_, f32[576,768]{1,0:T(8,128)} %get-tuple-element.67.refs_2_, ...), custom_call_target="tpu_custom_call" | custom-call | tf_op jit(solution)/shard_map/tail/pallas_call | solution.py:1109
  305.4 5.1 %finish.1 = (bf16[1,288,768]{2,1,0:T(8,128)(2,1)}, bf16[1,288,768]{2,1,0:T(8,128)(2,1)}, f32[1,3,192,192]{3,2,1,0:T(8,128)}, f32[1,192,192]{2,1,0:T(8,128)}, f32...) custom-call(bf16[12,192,384]{2,1,0:T(8,128)(2,1)} %get-tuple-element, ...), custom_call_target="tpu_custom_call" | custom-call | tf_op jit(solution)/shard_map/finish/pallas_call | solution.py:2129
